TPU v7x, 32 devices: a whole 2x2x4 slice. The times are simulated.
32 devices in a mesh: group: 2 (over core), expert: 8 (over z, y), dp: 2 (over x).
Axes of the slice: x: 2, y: 2, z: 4, core: 2. Of those that a mesh axis runs over, the one named last changes fastest.
Arguments:
- tokens: bfloat16 [512, 5120], P(('group', 'expert'), 'dp'), may hold values from -6 to 6
- grad_out: bfloat16 [512, 5120], P(('group', 'expert'), 'dp'), may hold values from -6 to 6
- expert_ids: int32 [512, 8], replicated, may hold values from 0 to 15, as said below
- gate_score: float32 [512, 8], replicated, may hold values from -6 to 6
- w_gate_up: bfloat16 [16, 5120, 2, 1024], P(('group', 'expert'), 'dp'), may hold values from -0.078125 to 0.078125
- w_down: bfloat16 [16, 1024, 5120], P(('group', 'expert'), None, 'dp'), may hold values from -0.1875 to 0.1875
Outputs:
- layer_out: bfloat16 [512, 5120], P(('group', 'expert'), 'dp')
- grad_in: bfloat16 [512, 5120], P(('group', 'expert'), 'dp')
Inputs may be any that keep to these rules, and one draw needn't show every extreme that they name: `expert_ids`: each row names 8 distinct experts, expert number = group * 8 + index, lying in exactly 1 group with 8 experts in each, listed by rising group. In every aligned block of 32 rows each group is named by exactly half of the rows. For a group g and an index e, among the rows of the blocks numbered j * 8 + e (j from 0 to 1) that name group g, no expert of g is named more than 32 times, and some expert of g exactly 32 times.
All inputs are finite; a program needn't handle non-finite values.
Results may differ from a plain program's by a relative error of at most 0.0057.
Values may be sent and summed in bfloat16 or wider, within the bound.
A program may use at most 64 MiB of HBM per device.

v0:
```python
import jax
import jax.numpy as jnp
from jax import lax
from jax.sharding import PartitionSpec as P

HIGHEST = lax.Precision.HIGHEST


def route_weights(gate_score):
    sigmoid_score = jax.nn.sigmoid(gate_score)
    return 2.5 * sigmoid_score / jnp.sum(sigmoid_score, axis=1, keepdims=True)


def slot_matrix(marked, places):
    running = jnp.cumsum(marked.astype(jnp.int32), axis=-2) - 1
    slot_range = jnp.arange(places, dtype=jnp.int32)
    matched = marked[..., None] & (running[..., None] == slot_range)
    return jnp.moveaxis(matched, -3, -1).astype(jnp.float32)


def local_grad(gate_pre, up_pre, hidden_grad):
    sigmoid_gate = jax.nn.sigmoid(gate_pre)
    gate_grad = hidden_grad * up_pre * sigmoid_gate * (1.0 + gate_pre * (1.0 - sigmoid_gate))
    up_grad = hidden_grad * gate_pre * sigmoid_gate
    return jnp.stack([gate_grad, up_grad], axis=1).astype(jnp.bfloat16)


def across(blocks):
    return lax.all_to_all(blocks, "group", split_axis=0, concat_axis=0, tiled=True)


def within(blocks):
    return lax.all_to_all(blocks, "expert", split_axis=0, concat_axis=0, tiled=True)


def share_sum(partial_value):
    return lax.psum_scatter(partial_value, "dp", scatter_dimension=2, tiled=True)


def share_fold(shares, step_fn, start_value):
    return step_fn(start_value, lax.all_gather(shares, "dp", axis=2, tiled=True), jnp.int32(0))


def on_device(tokens, grad_out, expert_ids, gate_score, w_gate_up, w_down):
    groups = lax.axis_size("group")
    members = lax.axis_size("expert")
    my_group = lax.axis_index("group")
    my_index = lax.axis_index("expert")
    per_column = tokens.shape[0]
    features = tokens.shape[1]
    visitors = per_column // 2
    top_count = expert_ids.shape[1]
    arrivals = groups * visitors
    capacity = min(arrivals, (3 * per_column * top_count + 2 * members - 1) // (2 * members))
    expert_rows = members * capacity
    weights = route_weights(gate_score).reshape(groups, members, per_column, top_count)
    pick_ids = expert_ids.reshape(groups, members, per_column, top_count)
    group_range = jnp.arange(groups, dtype=jnp.int32)
    my_picks = pick_ids[my_group, my_index]
    visits_mine = jnp.any(my_picks[:, :, None] // members == group_range, axis=1)
    leave_table = slot_matrix(visits_mine, visitors).astype(jnp.bfloat16)
    visits_here = jnp.any(pick_ids // members == my_group, axis=3)
    arrival_table = slot_matrix(visits_here[..., None], visitors)[:, :, 0]
    row_ids = jnp.einsum(
        "gest,getk->gesk", arrival_table, pick_ids.astype(jnp.float32), precision=HIGHEST
    )
    row_weights = jnp.einsum("gest,getk->gesk", arrival_table, weights, precision=HIGHEST)
    targets = (my_group * members + jnp.arange(members, dtype=jnp.int32)).astype(jnp.float32)
    matched = row_ids[..., None] == targets
    picked = jnp.any(matched, axis=3)
    picked_weight = jnp.sum(jnp.where(matched, row_weights[..., None], 0.0), axis=3)
    send_flags = picked[:, my_index].reshape(arrivals, members)
    send_table = slot_matrix(send_flags, capacity)
    send_share = jnp.transpose(picked_weight[:, my_index].reshape(arrivals, members))
    send_weight = send_table * send_share[:, None, :]
    came_flags = jnp.transpose(picked[:, :, :, my_index], (1, 0, 2)).reshape(members, arrivals)
    came_table = slot_matrix(came_flags[..., None], capacity)[:, 0]
    came_share = jnp.transpose(picked_weight[:, :, :, my_index], (1, 0, 2)).reshape(
        members, arrivals
    )
    slot_weight = jnp.einsum("ecr,er->ec", came_table, came_share, precision=HIGHEST).reshape(
        expert_rows
    )

    def dispatch(values):
        leaving = jnp.einsum(
            "gst,tf->gsf", leave_table, values, preferred_element_type=jnp.float32
        ).astype(jnp.bfloat16)
        arrived = across(leaving).reshape(arrivals, features)
        onward = jnp.einsum(
            "ecr,rf->ecf",
            send_table.astype(jnp.bfloat16),
            arrived,
            preferred_element_type=jnp.float32,
        ).astype(jnp.bfloat16)
        return within(onward).reshape(expert_rows, features)

    def combine(values, table):
        returned = within(values.reshape(members, capacity, features)).astype(jnp.float32)
        summed = jnp.einsum("ecr,ecf->rf", table, returned, precision=HIGHEST).astype(jnp.bfloat16)
        home = across(summed.reshape(groups, visitors, features))
        return jnp.einsum(
            "gst,gsf->tf", leave_table, home, preferred_element_type=jnp.float32
        ).astype(jnp.bfloat16)

    rows_in = dispatch(tokens)
    rows_grad = dispatch(grad_out)
    gate_weights = w_gate_up[0]
    down_weights = w_down[0]
    partial_value = jnp.einsum(
        "rf,fkh->rkh", rows_in, gate_weights, preferred_element_type=jnp.float32
    )
    grad_partial = jnp.einsum(
        "rf,hf->rh", rows_grad, down_weights, preferred_element_type=jnp.float32
    )
    empty_rows = jnp.zeros((expert_rows, features), jnp.float32)
    gate_both = share_sum(partial_value)
    gate_pre = gate_both[:, 0]
    up_pre = gate_both[:, 1]
    hidden = (jax.nn.silu(gate_pre) * up_pre).astype(jnp.bfloat16)[:, None, :]

    def down_step(running_sum, gathered, first_row):
        return jnp.dot(gathered[:, 0], down_weights, preferred_element_type=jnp.float32)

    expert_out = share_fold(hidden, down_step, empty_rows).astype(jnp.bfloat16)
    hidden_grad = share_sum(grad_partial[:, None, :])[:, 0] * slot_weight[:, None]
    pre_grad = local_grad(gate_pre, up_pre, hidden_grad)

    def input_step(running_sum, gathered, first_row):
        return jnp.einsum("rkh,fkh->rf", gathered, gate_weights, preferred_element_type=jnp.float32)

    expert_grad = share_fold(pre_grad, input_step, empty_rows).astype(jnp.bfloat16)
    layer_out = combine(expert_out, send_weight)
    grad_in = combine(expert_grad, send_table)
    return (layer_out, grad_in)


def solution(mesh):
    return jax.shard_map(
        on_device,
        mesh=mesh,
        in_specs=(
            P(("group", "expert"), "dp"),
            P(("group", "expert"), "dp"),
            P(),
            P(),
            P(("group", "expert"), "dp", None, None),
            P(("group", "expert"), None, "dp"),
        ),
        out_specs=(P(("group", "expert"), "dp"), P(("group", "expert"), "dp")),
        check_vma=False,
    )
```

profile of v0, /device:TPU:0, one launch (start us, length us, event | category | flops | bytes accessed | tf_op | source)
XLA Modules:
  0.0 243.2 jit_solution(1665689895209812796)
XLA Ops:
  7.2 0.8 reshape.216
  8.3 0.1 copy.80
  8.4 0.1 copy.81
  8.5 0.9 convolution_convert_fusion.2
  9.3 3.4 %all-to-all-start.4 = ((bf16[2,16,2560]{2,1,0:T(8,128)(2,1)}), bf16[2,16,2560]{2,1,0:T(8,128)(2,1)S(1)}, u32[]{:S(2)}, u32[]{:S(2)}) async-start(bf16[2,16,2560]{2,1,0:T(8,128)(2,1)} %convolution_convert_fusion.2), calls=%async_computation.5 | async-start | bytes 327680 | tf_op jit(solution)/shard_map/all_to_all | solution.py:29
  12.8 0.7 fusion.66
  13.5 0.1 and.89
  13.6 0.4 reduce_window_sum.45
  14.0 0.2 fusion.33
  14.3 0.1 compare_reduce_fusion
  14.4 0.1 and.92
  14.5 0.1 copy.84
  14.7 0.8 convolution_convert_fusion.3
  15.6 3.4 %all-to-all-start = ((bf16[2,16,2560]{2,1,0:T(8,128)(2,1)}), bf16[2,16,2560]{2,1,0:T(8,128)(2,1)S(1)}, u32[]{:S(2)}, u32[]{:S(2)}) async-start(bf16[2,16,2560]{2,1,0:T(8,128)(2,1)} %convolution_convert_fusion.3), calls=%async_computation | async-start | bytes 327680 | tf_op jit(solution)/shard_map/all_to_all | solution.py:29
  19.0 1.7 convolution_convert_fusion
  20.8 7.3 %all-to-all-start.5 = ((bf16[8,32,2560]{2,1,0:T(8,128)(2,1)}), bf16[8,32,2560]{2,1,0:T(8,128)(2,1)S(1)}, u32[]{:S(2)}, u32[]{:S(2)}) async-start(bf16[8,32,2560]{2,1,0:T(8,128)(2,1)} %convolution_convert_fusion), calls=%async_computation.6 | async-start | bytes 2621440 | tf_op jit(solution)/shard_map/all_to_all | solution.py:33
  28.1 1.7 convolution_convert_fusion.1
  29.8 30.3 %all-to-all-done.5 = bf16[8,32,2560]{2,1,0:T(8,128)(2,1)S(1)} async-done(((bf16[8,32,2560]{2,1,0:T(8,128)(2,1)}), bf16[8,32,2560]{2,1,0:T(8,128)(2,1)S(1)}, u32[]{:S(2)}, u32[]{:S(2)}) %all-to-all-start.5) | async-done | bytes 1310752 | tf_op jit(solution)/shard_map/all_to_all | solution.py:33
  60.1 3.6 %all-to-all-start.1 = ((bf16[8,32,2560]{2,1,0:T(8,128)(2,1)}), bf16[8,32,2560]{2,1,0:T(8,128)(2,1)S(1)}, u32[]{:S(2)}, u32[]{:S(2)}) async-start(bf16[8,32,2560]{2,1,0:T(8,128)(2,1)} %convolution_convert_fusion.1), calls=%async_computation.1 | async-start | bytes 2621440 | tf_op jit(solution)/shard_map/all_to_all | solution.py:33
  63.8 5.0 %fusion.21 = f32[256,1,1024]{2,0,1:T(8,128)} fusion(bf16[256,2560]{1,0:T(8,128)(2,1)S(1)} %bitcast.119, bf16[1,1024,2560]{2,1,0:T(8,128)(2,1)} %param.11), kind=kOutput, calls=%fused_computation.23 | convolution fusion | flops 1342177280 | bytes 7602176 | tf_op jit(solution)/shard_map/rf,hf->rh/dot_general | solution.py:113
  68.9 26.5 %all-to-all-done.1 = bf16[8,32,2560]{2,1,0:T(8,128)(2,1)S(1)} async-done(((bf16[8,32,2560]{2,1,0:T(8,128)(2,1)}), bf16[8,32,2560]{2,1,0:T(8,128)(2,1)S(1)}, u32[]{:S(2)}, u32[]{:S(2)}) %all-to-all-start.1) | async-done | bytes 1310752 | tf_op jit(solution)/shard_map/all_to_all | solution.py:33
  95.3 8.7 %fusion.2 = f32[256,2,1024]{2,0,1:T(8,128)} fusion(bf16[256,2560,1]{1,0,2:T(8,128)(2,1)S(1)} %bitcast.118, bf16[2560,2,1024]{2,1,0:T(2,128)(2,1)} %bitcast.137), kind=kOutput, calls=%fused_computation.2 | convolution fusion | flops 2684354560 | bytes 13893632 | tf_op jit(solution)/shard_map/rf,fkh->rkh/dot_general | solution.py:110
  104.0 0.7 copy-done.2
  104.8 0.1 reshape.217
  104.9 0.1 and.96
  105.0 0.2 reduce_window_sum.47
  105.2 0.2 fusion.31
  105.4 0.1 fusion.24
  105.6 0.1 reshape.234
  105.7 0.2 fusion.40
  105.9 0.1 mul.69
  106.0 29.2 %reduce-scatter.3.cloned.1.call-done = f32[256,2,512]{2,0,1:T(8,128)} async-done(((f32[256,2,1024]{2,0,1:T(8,128)}), f32[256,2,512]{2,0,1:T(8,128)}) %reduce-scatter.3.cloned.1.call-update) | async-done | bytes 1048592 | tf_op jit(solution)/shard_map/reduce_scatter | solution.py:37
  135.2 1.7 multiply_convert_fusion.1
  136.8 8.6 %all_gather.6 = bf16[256,1,1024]{2,0,1:T(8,128)(2,1)S(1)} all-gather(bf16[256,1,512]{2,0,1:T(8,128)(2,1)S(1)} %get-tuple-element.4), channel_id=1, replica_groups=mesh['group'=2,'expert'=8,'dp'=2] {'dp'}, dimensions={2}, use_global_device_ids=true | all-gather | bytes 786432 | tf_op jit(solution)/shard_map/all_gather | solution.py:41
  145.4 5.1 %fusion.14 = bf16[256,2560]{1,0:T(8,128)(2,1)} fusion(bf16[1,1024,2560]{2,1,0:T(8,128)(2,1)} %param.11, bf16[256,1,1024]{2,0,1:T(8,128)(2,1)S(1)} %all_gather.6), kind=kOutput, calls=%fused_computation.12 | convolution fusion | flops 1342832640 | bytes 7077888 | tf_op jit(solution)/shard_map/dot_general | solution.py:123
  150.5 5.5 %all-to-all-start.2 = ((bf16[8,32,2560]{2,1,0:T(8,128)(2,1)}), bf16[8,32,2560]{2,1,0:T(8,128)(2,1)S(1)}, u32[]{:S(2)}, u32[]{:S(2)}) async-start(bf16[8,32,2560]{2,1,0:T(8,128)(2,1)} %bitcast.17), calls=%async_computation.3 | async-start | bytes 2621440 | tf_op jit(solution)/shard_map/all_to_all | solution.py:33
  156.0 0.2 all-gather.2.cloned.1.call-start
  156.2 0.9 pad_maximum_fusion
  157.2 22.9 %all-gather.2.cloned.1.call-done = bf16[256,2,1024]{2,0,1:T(8,128)(2,1)} async-done(((bf16[256,2,512]{2,0,1:T(8,128)(2,1)}), bf16[256,2,1024]{2,0,1:T(8,128)(2,1)}) %all-gather.2.cloned.1.call-update) | async-done | bytes 1048592 | tf_op jit(solution)/shard_map/all_gather | solution.py:41
  180.1 8.9 %fusion.11 = bf16[256,2560]{1,0:T(8,128)(2,1)} fusion(bf16[256,2,1024]{2,0,1:T(8,128)(2,1)} %all-gather.2.cloned.1.call-done, bf16[2560,2,1024]{2,1,0:T(2,128)(2,1)} %bitcast.138), kind=kOutput, calls=%fused_computation.11 | convolution fusion | flops 2685009920 | bytes 12845056 | tf_op jit(solution)/shard_map/rkh,fkh->rf/dot_general | solution.py:130
  189.0 1.3 fusion.17
  190.3 3.8 %all_to_all.40 = bf16[2,16,2560]{2,1,0:T(8,128)(2,1)S(1)} all-to-all(bf16[2,16,2560]{2,1,0:T(8,128)(2,1)S(1)} %bitcast.123), channel_id=1, replica_groups=mesh['group'=2,'expert'=8,'dp'=2] {'group'}, dimensions={0} | all-to-all | bytes 327680 | tf_op jit(solution)/shard_map/all_to_all | solution.py:29
  194.2 5.5 %all-to-all-start.6 = ((bf16[8,32,2560]{2,1,0:T(8,128)(2,1)}), bf16[8,32,2560]{2,1,0:T(8,128)(2,1)S(1)}, u32[]{:S(2)}, u32[]{:S(2)}) async-start(bf16[8,32,2560]{2,1,0:T(8,128)(2,1)} %bitcast.35), calls=%async_computation.8 | async-start | bytes 2621440 | tf_op jit(solution)/shard_map/all_to_all | solution.py:33
  199.7 0.9 fusion.18
  200.6 30.8 %all-to-all-done.6 = bf16[8,32,2560]{2,1,0:T(8,128)(2,1)S(1)} async-done(((bf16[8,32,2560]{2,1,0:T(8,128)(2,1)}), bf16[8,32,2560]{2,1,0:T(8,128)(2,1)S(1)}, u32[]{:S(2)}, u32[]{:S(2)}) %all-to-all-start.6) | async-done | bytes 1310752 | tf_op jit(solution)/shard_map/all_to_all | solution.py:33
  231.4 0.5 fusion.19
  231.9 3.8 %all_to_all.41 = bf16[2,16,2560]{2,1,0:T(8,128)(2,1)S(1)} all-to-all(bf16[2,16,2560]{2,1,0:T(8,128)(2,1)S(1)} %bitcast.122), channel_id=1, replica_groups=mesh['group'=2,'expert'=8,'dp'=2] {'group'}, dimensions={0} | all-to-all | bytes 327680 | tf_op jit(solution)/shard_map/all_to_all | solution.py:29
  235.7 0.9 fusion.20
  (43 shorter events, 0.8 us)
Async XLA Ops:
  7.2 1.3 copy-start
  7.2 7.6 %copy-start.1 = (bf16[32,2560]{1,0:T(8,128)(2,1)S(1)}, bf16[32,2560]{1,0:T(8,128)(2,1)}, u32[]{:S(2)}) copy-start(bf16[32,2560]{1,0:T(8,128)(2,1)} %param.6) | copy-start | bytes 491524
  9.3 6.3 %all-to-all-start.4 = ((bf16[2,16,2560]{2,1,0:T(8,128)(2,1)}), bf16[2,16,2560]{2,1,0:T(8,128)(2,1)S(1)}, u32[]{:S(2)}, u32[]{:S(2)}) async-start(bf16[2,16,2560]{2,1,0:T(8,128)(2,1)} %convolution_convert_fusion.2), calls=%async_computation.5 | async-start | bytes 327680 | tf_op jit(solution)/shard_map/all_to_all | solution.py:29
  15.6 5.2 %all-to-all-start = ((bf16[2,16,2560]{2,1,0:T(8,128)(2,1)}), bf16[2,16,2560]{2,1,0:T(8,128)(2,1)S(1)}, u32[]{:S(2)}, u32[]{:S(2)}) async-start(bf16[2,16,2560]{2,1,0:T(8,128)(2,1)} %convolution_convert_fusion.3), calls=%async_computation | async-start | bytes 327680 | tf_op jit(solution)/shard_map/all_to_all | solution.py:29
  20.8 39.4 %all-to-all-start.5 = ((bf16[8,32,2560]{2,1,0:T(8,128)(2,1)}), bf16[8,32,2560]{2,1,0:T(8,128)(2,1)S(1)}, u32[]{:S(2)}, u32[]{:S(2)}) async-start(bf16[8,32,2560]{2,1,0:T(8,128)(2,1)} %convolution_convert_fusion), calls=%async_computation.6 | async-start | bytes 2621440 | tf_op jit(solution)/shard_map/all_to_all | solution.py:33
  60.1 35.2 %all-to-all-start.1 = ((bf16[8,32,2560]{2,1,0:T(8,128)(2,1)}), bf16[8,32,2560]{2,1,0:T(8,128)(2,1)S(1)}, u32[]{:S(2)}, u32[]{:S(2)}) async-start(bf16[8,32,2560]{2,1,0:T(8,128)(2,1)} %convolution_convert_fusion.1), calls=%async_computation.1 | async-start | bytes 2621440 | tf_op jit(solution)/shard_map/all_to_all | solution.py:33
  63.7 42.3 %reduce-scatter.5.cloned.1.call-start = ((), (), s32[]{:S(2)}) async-start(), calls=%async_computation.11 | async-start | bytes 1572864 | tf_op jit(solution)/shard_map/reduce_scatter | solution.py:37
  68.8 66.3 %reduce-scatter.3.cloned.1.call-start = ((), (), s32[]{:S(2)}) async-start(), calls=%async_computation.10 | async-start | bytes 3145728 | tf_op jit(solution)/shard_map/reduce_scatter | solution.py:37
  104.0 0.7 copy-start.2
  150.5 38.6 %all-to-all-start.2 = ((bf16[8,32,2560]{2,1,0:T(8,128)(2,1)}), bf16[8,32,2560]{2,1,0:T(8,128)(2,1)S(1)}, u32[]{:S(2)}, u32[]{:S(2)}) async-start(bf16[8,32,2560]{2,1,0:T(8,128)(2,1)} %bitcast.17), calls=%async_computation.3 | async-start | bytes 2621440 | tf_op jit(solution)/shard_map/all_to_all | solution.py:33
  156.0 24.1 %all-gather.2.cloned.1.call-start = ((), (), s32[]{:S(2)}) async-start(), calls=%async_computation.12 | async-start | bytes 1572864 | tf_op jit(solution)/shard_map/all_gather | solution.py:41
  194.2 37.2 %all-to-all-start.6 = ((bf16[8,32,2560]{2,1,0:T(8,128)(2,1)}), bf16[8,32,2560]{2,1,0:T(8,128)(2,1)S(1)}, u32[]{:S(2)}, u32[]{:S(2)}) async-start(bf16[8,32,2560]{2,1,0:T(8,128)(2,1)} %bitcast.35), calls=%async_computation.8 | async-start | bytes 2621440 | tf_op jit(solution)/shard_map/all_to_all | solution.py:33
Sparse Core Ops, SparseCore 0:
  69.0 21.7 reduce-scatter.4
  104.2 30.9 reduce-scatter.2
  158.3 21.7 all-gather.1
where the time goes:
time: 244 us; the launch traced here: 243 us
  waiting for transfers between devices  140 us (57%)
  matrix products  37.1 us (15%)
  starting transfers between devices  29.1 us (12%)
  blocking collectives  16.2 us (7%)
  between operations  13.9 us (6%)
  other arithmetic  4.38 us (2%)
  local copies, waits for them, and re-layouts  2.68 us (1%)
    all_to_all x4, waiting for transfers between devices, within(): lax.all_to_all(blocks, 'expert', split_axis=0, concat_axis=0, tiled=True)  87.6 us
    reduce_scatter x2, waiting for transfers between devices, share_sum(): lax.psum_scatter(partial_value, 'dp', scatter_dimension=2, tiled=True)  29.2 us
    all_gather x1, waiting for transfers between devices, share_fold(): lax.all_gather(shares, 'dp', axis=2, tiled=True)  22.9 us
    all_to_all x4, starting transfers between devices, within(): lax.all_to_all(blocks, 'expert', split_axis=0, concat_axis=0, tiled=True)  22 us
    dot_general x1, matrix products, input_step(): jnp.einsum('rkh,fkh->rf', gathered, gate_weights, preferred_element_type=...  8.93 us
    dot_general x1, matrix products, on_device(): jnp.einsum('rf,fkh->rkh', rows_in, gate_weights, preferred_element_type=j...  8.68 us
    all_gather x1, blocking collectives, share_fold(): lax.all_gather(shares, 'dp', axis=2, tiled=True)  8.56 us
    all_to_all x2, blocking collectives, across(): lax.all_to_all(blocks, 'group', split_axis=0, concat_axis=0, tiled=True)  7.69 us
  transfers between devices with their start and end apart: 9, of which 5 were waited for; matrix products, arithmetic and copies ran while one was open for 13% of the time, Pallas kernels for 0%

commit v1 on v0

--- a/solution.py
+++ b/solution.py
@@ -39,6 +39,78 @@
 
 def share_fold(shares, step_fn, start_value):
     return step_fn(start_value, lax.all_gather(shares, "dp", axis=2, tiled=True), jnp.int32(0))
+
+
+def dense_device(tokens, grad_out, expert_ids, gate_score, w_gate_up, w_down):
+    groups = lax.axis_size("group")
+    members = lax.axis_size("expert")
+    shares = lax.axis_size("dp")
+    my_group = lax.axis_index("group")
+    my_index = lax.axis_index("expert")
+    per_column, features = tokens.shape
+    visitors = per_column // groups
+    arrivals = groups * visitors
+    expert_rows = members * arrivals
+    top_count = expert_ids.shape[1]
+    weights = route_weights(gate_score)
+    my_expert = my_group * members + my_index
+    share = jnp.sum(jnp.where(expert_ids == my_expert, weights, 0.0), axis=1)
+    token_group = (expert_ids[:, 0] // members).reshape(groups, members, per_column)
+    here = token_group == my_group
+    arrival_table = slot_matrix(here[..., None], visitors)[:, :, 0]
+    row_share = jnp.sum(
+        arrival_table * share.reshape(groups, members, 1, per_column), axis=3
+    )
+    row_share = jnp.transpose(row_share, (1, 0, 2)).reshape(expert_rows, 1)
+    group_range = jnp.arange(groups, dtype=jnp.int32)
+    visits_mine = token_group[my_group, my_index][:, None] == group_range
+    leave_table = slot_matrix(visits_mine, visitors).astype(jnp.bfloat16)
+    gate_weights = w_gate_up[0]
+    down_weights = w_down[0]
+
+    both = jnp.concatenate([tokens, grad_out], axis=1)
+    leaving = jnp.einsum(
+        "gst,tf->gsf", leave_table, both, preferred_element_type=jnp.float32
+    ).astype(jnp.bfloat16)
+    arrived = across(leaving).reshape(arrivals, 2 * features)
+    rows_in = lax.all_gather(arrived[:, :features], "expert", axis=0, tiled=True)
+    rows_grad = lax.all_gather(arrived[:, features:], "expert", axis=0, tiled=True)
+
+    swap = [(i, (i + 1) % shares) for i in range(shares)]
+
+    def dp_sum(value):
+        total = value
+        moving = value.astype(jnp.bfloat16)
+        for _ in range(shares - 1):
+            moving = lax.ppermute(moving, "dp", swap)
+            total = total + moving.astype(jnp.float32)
+        return total
+
+    gate_both = dp_sum(
+        jnp.einsum("rf,fkh->rkh", rows_in, gate_weights, preferred_element_type=jnp.float32)
+    )
+    grad_sum = dp_sum(
+        jnp.einsum("rf,hf->rh", rows_grad, down_weights, preferred_element_type=jnp.float32)
+    )
+    gate_pre = gate_both[:, 0]
+    up_pre = gate_both[:, 1]
+    hidden = (jax.nn.silu(gate_pre) * up_pre).astype(jnp.bfloat16)
+    expert_out = jnp.dot(hidden, down_weights, preferred_element_type=jnp.float32)
+    out_part = (expert_out * row_share).astype(jnp.bfloat16)
+    pre_grad = local_grad(gate_pre, up_pre, grad_sum * row_share)
+    grad_part = jnp.einsum(
+        "rkh,fkh->rf", pre_grad, gate_weights, preferred_element_type=jnp.float32
+    ).astype(jnp.bfloat16)
+    out_sum = lax.psum_scatter(out_part, "expert", scatter_dimension=0, tiled=True)
+    grad_total = lax.psum_scatter(grad_part, "expert", scatter_dimension=0, tiled=True)
+
+    def give_back(summed):
+        home = across(summed.reshape(groups, visitors, features))
+        return jnp.einsum(
+            "gst,gsf->tf", leave_table, home, preferred_element_type=jnp.float32
+        ).astype(jnp.bfloat16)
+
+    return (give_back(out_sum), give_back(grad_total))
 
 
 def on_device(tokens, grad_out, expert_ids, gate_score, w_gate_up, w_down):
@@ -135,9 +207,15 @@
     return (layer_out, grad_in)
 
 
+def per_device(tokens, grad_out, expert_ids, gate_score, w_gate_up, w_down):
+    dense = expert_ids.shape[1] == lax.axis_size("expert")
+    plan = dense_device if dense else on_device
+    return plan(tokens, grad_out, expert_ids, gate_score, w_gate_up, w_down)
+
+
 def solution(mesh):
     return jax.shard_map(
-        on_device,
+        per_device,
         mesh=mesh,
         in_specs=(
             P(("group", "expert"), "dp"),

time: 244 us -> 250 us (1.025)
  waiting for transfers between devices: 140 us -> 184 us
  starting transfers between devices: 29.1 us -> 6.58 us
  blocking collectives: 16.2 us -> 8.89 us
  matrix products: 37.1 us -> 30.4 us
    all_to_all x4 -> x0, waiting for transfers between devices: 87.6 us -> none  [within(): lax.all_to_all(blocks, 'expert', split_axis=0, concat_axis=0, tiled=True)]
    reduce_scatter x2, waiting for transfers between devices: 29.2 us -> 103 us  [the longest x1 62.3 us: dense_device(): lax.psum_scatter(grad_part, 'expert', scatter_dimension=0, tiled=True)]
    ppermute x0 -> x2, waiting for transfers between devices: none -> 32.9 us  [dp_sum(): moving = lax.ppermute(moving, 'dp', swap)]
    all_gather x1 -> x2, waiting for transfers between devices: 22.9 us -> 47.1 us  [the longest x1 43.9 us: dense_device(): lax.all_gather(arrived[:, :features], 'expert', axis=0, tiled=True)]
    all_to_all x4 -> x0, starting transfers between devices: 22 us -> none  [within(): lax.all_to_all(blocks, 'expert', split_axis=0, concat_axis=0, tiled=True)]
    all_gather x1 -> x0, blocking collectives: 8.56 us -> none  [share_fold(): lax.all_gather(shares, 'dp', axis=2, tiled=True)]
    dot_general x15 -> x7, matrix products: 37.1 us -> 30.4 us  [the longest x1 9.14 us: dense_device(): jnp.einsum('rf,fkh->rkh', rows_in, gate_weights, preferred_element_type=j...]
    all_to_all x2 -> x1, starting transfers between devices: 6.85 us -> 3.42 us  [across(): lax.all_to_all(blocks, 'group', split_axis=0, concat_axis=0, tiled=True)]
  transfers between devices with their start and end apart: 9 -> 7, of which waited for: 5 -> 7; matrix products, arithmetic and copies ran while one was open for 13% -> 13% of each run, Pallas kernels for 0% -> 0%
where the time goes in v1:
time: 250 us; the launch traced here: 249 us
  waiting for transfers between devices  184 us (74%)
  matrix products  30.4 us (12%)
  between operations  13.8 us (6%)
  blocking collectives  8.89 us (4%)
  starting transfers between devices  6.58 us (3%)
  other arithmetic  3.34 us (1%)
    reduce_scatter x1, waiting for transfers between devices, dense_device(): lax.psum_scatter(grad_part, 'expert', scatter_dimension=0, tiled=True)  62.3 us
    all_gather x1, waiting for transfers between devices, dense_device(): lax.all_gather(arrived[:, :features], 'expert', axis=0, tiled=True)  43.9 us
    reduce_scatter x1, waiting for transfers between devices, dense_device(): lax.psum_scatter(out_part, 'expert', scatter_dimension=0, tiled=True)  40.7 us
    ppermute x2, waiting for transfers between devices, dp_sum(): moving = lax.ppermute(moving, 'dp', swap)  32.9 us
    dot_general x1, matrix products, dense_device(): jnp.einsum('rf,fkh->rkh', rows_in, gate_weights, preferred_element_type=j...  9.14 us
    all_to_all x2, blocking collectives, across(): lax.all_to_all(blocks, 'group', split_axis=0, concat_axis=0, tiled=True)  8.89 us
    dot_general x1, matrix products, dense_device(): jnp.einsum('rkh,fkh->rf', pre_grad, gate_weights, preferred_element_type=...  8.65 us
    dot_general x1, matrix products, dense_device(): jnp.dot(hidden, down_weights, preferred_element_type=jnp.float32)  5.18 us
  transfers between devices with their start and end apart: 7, of which 7 were waited for; matrix products, arithmetic and copies ran while one was open for 13% of the time, Pallas kernels for 0%

profile of v1, /device:TPU:0, one launch (start us, length us, event | category | flops | bytes accessed | tf_op | source)
XLA Modules:
  0.0 249.3 jit_solution(8328399638847612313)
XLA Ops:
  7.2 0.0 all-gather.3.cloned.1.call-start
  7.2 0.7 slice_reduce_fusion
  7.9 0.1 squeeze.19
  8.1 0.1 fusion.42
  8.1 0.1 reduce_window_sum.22
  8.2 0.1 copy.14
  8.3 1.2 convolution_convert_fusion
  9.5 4.0 %all_to_all.15 = bf16[2,16,5120]{2,1,0:T(8,128)(2,1)S(1)} all-to-all(bf16[2,16,5120]{2,1,0:T(8,128)(2,1)S(1)} %convolution_convert_fusion), channel_id=1, replica_groups=mesh['group'=2,'expert'=8,'dp'=2] {'group'}, dimensions={0} | all-to-all | bytes 655360 | tf_op jit(solution)/shard_map/all_to_all | solution.py:29
  13.5 0.7 fusion.57
  14.3 0.0 all-gather.3.cloned.1.call-update
  14.3 0.0 all-gather.5.cloned.1.call-start
  14.3 0.7 all-gather.5.cloned.1.call-update
  15.0 0.0 reduce-scatter.3.cloned.1.call-start
  15.1 43.9 %all-gather.3.cloned.1.call-done = bf16[256,2560]{1,0:T(8,128)(2,1)} async-done(((bf16[32,2560]{1,0:T(8,128)(2,1)}), bf16[256,2560]{1,0:T(8,128)(2,1)}) %all-gather.3.cloned.1.call-update) | async-done | bytes 1310736 | tf_op jit(solution)/shard_map/all_gather | solution.py:76
  59.0 0.0 copy-start
  59.0 0.0 copy-start.1
  59.0 9.1 %fusion.58 = (bf16[256,2,1024]{2,0,1:T(8,128)(2,1)S(1)}, f32[256,2,1024]{2,0,1:T(8,128)}) fusion(bf16[2560,2,1024]{2,1,0:T(2,128)(2,1)} %bitcast.96, bf16[256,2560]{1,0:T(8,128)(2,1)} %all-gather.3.cloned.1.call-done), kind=kOutput, calls=%fused_computation.79 | convolution fusion | flops 2684878848 | bytes 14942208 | tf_op jit(solution)/shard_map/rf,fkh->rkh/dot_general | solution.py:90
  68.1 1.5 collective-permute-start
  69.6 0.0 copy-done
  69.6 0.0 copy-done.1
  69.7 0.1 mul.69
  69.7 0.4 reduce_window_sum.23
  70.1 0.1 select_reduce_fusion
  70.3 0.1 mul.72
  70.3 21.7 %collective-permute-done = bf16[256,2,1024]{2,0,1:T(8,128)(2,1)S(1)} collective-permute-done((bf16[256,2,1024]{2,0,1:T(8,128)(2,1)S(1)}, bf16[256,2,1024]{2,0,1:T(8,128)(2,1)S(1)}, u32[]{:S(2)}, u32[]{:S(2)}) %collective-permute-start) | collective-permute-done | bytes 1048608 | tf_op jit(solution)/shard_map/ppermute | solution.py:85
  92.0 1.9 convert_add_fusion
  93.9 5.2 %fusion.17 = bf16[256,2560]{1,0:T(8,128)(2,1)} fusion(bf16[1,1024,2560]{2,1,0:T(8,128)(2,1)} %param.11, f32[256]{0:T(256)S(1)} %mul.72, f32[256,2,1024]{2,0,1:T(8,128)S(1)} %convert_add_fusion), kind=kOutput, calls=%fused_computation.12 | convolution fusion | flops 1345060864 | bytes 8651776 | tf_op jit(solution)/shard_map/dot_general | solution.py:98
  99.1 0.0 reduce-scatter.3.cloned.1.call-update
  99.1 0.0 reduce-scatter.5.cloned.1.call-start
  99.2 3.3 %all-gather.5.cloned.1.call-done = bf16[256,2560]{1,0:T(8,128)(2,1)} async-done(((bf16[32,2560]{1,0:T(8,128)(2,1)}), bf16[256,2560]{1,0:T(8,128)(2,1)}) %all-gather.5.cloned.1.call-update) | async-done | bytes 1310736 | tf_op jit(solution)/shard_map/all_gather | solution.py:77
  102.4 4.4 %fusion.59 = (bf16[256,1024]{1,0:T(8,128)(2,1)S(1)}, f32[256,1024]{1,0:T(8,128)S(1)}) fusion(bf16[256,2560]{1,0:T(8,128)(2,1)} %all-gather.5.cloned.1.call-done, bf16[1,1024,2560]{2,1,0:T(8,128)(2,1)} %param.11), kind=kOutput, calls=%fused_computation.80 | convolution fusion | flops 1342439424 | bytes 8126464 | tf_op jit(solution)/shard_map/rf,hf->rh/dot_general | solution.py:93
  106.9 1.5 collective-permute-start.1
  108.4 11.2 %collective-permute-done.1 = bf16[256,1024]{1,0:T(8,128)(2,1)S(1)} collective-permute-done((bf16[256,1024]{1,0:T(8,128)(2,1)S(1)}, bf16[256,1024]{1,0:T(8,128)(2,1)S(1)}, u32[]{:S(2)}, u32[]{:S(2)}) %collective-permute-start.1) | collective-permute-done | bytes 524320 | tf_op jit(solution)/shard_map/ppermute | solution.py:85
  119.6 0.7 fusion.37
  120.3 8.7 %fusion.14 = bf16[256,2560]{1,0:T(8,128)(2,1)} fusion(bf16[2560,2,1024]{2,1,0:T(2,128)(2,1)} %bitcast.97, bf16[256,1,1024]{2,0,1:T(8,128)(2,1)S(1)} %get-tuple-element.6, bf16[256,1,1024]{2,0,1:T(8,128)(2,1)S(1)} %get-tuple-element.5), kind=kOutput, calls=%fused_computation.11 | convolution fusion | flops 2685534208 | bytes 12845056 | tf_op jit(solution)/shard_map/rkh,fkh->rf/dot_general | solution.py:101
  129.0 0.0 reduce-scatter.5.cloned.1.call-update
  129.0 40.7 %reduce-scatter.3.cloned.1.call-done = bf16[32,2560]{1,0:T(8,128)(2,1)} async-done(((bf16[256,2560]{1,0:T(8,128)(2,1)}), bf16[32,2560]{1,0:T(8,128)(2,1)}) %reduce-scatter.3.cloned.1.call-update) | async-done | bytes 163856 | tf_op jit(solution)/shard_map/reduce_scatter | solution.py:104
  169.8 4.9 %all_to_all.16 = bf16[2,16,2560]{2,1,0:T(8,128)(2,1)S(1)} all-to-all(bf16[2,16,2560]{2,1,0:T(8,128)(2,1)} %bitcast.93), channel_id=1, replica_groups=mesh['group'=2,'expert'=8,'dp'=2] {'group'}, dimensions={0} | all-to-all | bytes 327680 | tf_op jit(solution)/shard_map/all_to_all | solution.py:29
  174.6 62.3 %reduce-scatter.5.cloned.1.call-done = bf16[32,2560]{1,0:T(8,128)(2,1)} async-done(((bf16[256,2560]{1,0:T(8,128)(2,1)}), bf16[32,2560]{1,0:T(8,128)(2,1)}) %reduce-scatter.5.cloned.1.call-update) | async-done | bytes 163856 | tf_op jit(solution)/shard_map/reduce_scatter | solution.py:105
  237.0 3.4 %all-to-all-start.2 = ((bf16[2,16,2560]{2,1,0:T(8,128)(2,1)}), bf16[2,16,2560]{2,1,0:T(8,128)(2,1)S(1)}, u32[]{:S(2)}, u32[]{:S(2)}) async-start(bf16[2,16,2560]{2,1,0:T(8,128)(2,1)} %bitcast.94), calls=%async_computation.4 | async-start | bytes 327680 | tf_op jit(solution)/shard_map/all_to_all | solution.py:29
  240.4 0.9 fusion.20
  241.3 0.6 all-to-all-done.2
  241.9 0.9 fusion.21
  (8 shorter events, 0.1 us)
Async XLA Ops:
  7.2 51.8 %all-gather.3.cloned.1.call-start = ((), (), s32[]{:S(2)}) async-start(), calls=%async_computation.5 | async-start | bytes 1474560 | tf_op jit(solution)/shard_map/all_gather | solution.py:76
  14.3 88.2 %all-gather.5.cloned.1.call-start = ((), (), s32[]{:S(2)}) async-start(), calls=%async_computation.7 | async-start | bytes 1474560 | tf_op jit(solution)/shard_map/all_gather | solution.py:77
  15.0 154.7 %reduce-scatter.3.cloned.1.call-start = ((), (), s32[]{:S(2)}) async-start(), calls=%async_computation.6 | async-start | bytes 1474560 | tf_op jit(solution)/shard_map/reduce_scatter | solution.py:104
  59.0 10.6 %copy-start = (f32[512,8]{0,1:T(8,128)S(1)}, f32[512,8]{0,1:T(8,128)}, u32[]{:S(2)}) copy-start(f32[512,8]{0,1:T(8,128)} %param.9) | copy-start | bytes 49156
  59.0 10.6 %copy-start.1 = (s32[512,8]{0,1:T(8,128)S(1)}, s32[512,8]{0,1:T(8,128)}, u32[]{:S(2)}) copy-start(s32[512,8]{0,1:T(8,128)} %param.8) | copy-start | bytes 49156
  68.1 23.9 %collective-permute-start = (bf16[256,2,1024]{2,0,1:T(8,128)(2,1)S(1)}, bf16[256,2,1024]{2,0,1:T(8,128)(2,1)S(1)}, u32[]{:S(2)}, u32[]{:S(2)}) collective-permute-start(bf16[256,2,1024]{2,0,1:T(8,128)(2,1)S(1)} %get-tuple-element.9), channel_id=1, source_target_pairs={{0,1},{1,0},{2,3},{3,2},{4,5},{5,4},{6,7},{7,6},{8,9},{9,8},{10,11... | collective-permute-start | bytes 3145736 | tf_op jit(solution)/shard_map/ppermute | solution.py:85
  99.1 137.8 %reduce-scatter.5.cloned.1.call-start = ((), (), s32[]{:S(2)}) async-start(), calls=%async_computation.8 | async-start | bytes 1474560 | tf_op jit(solution)/shard_map/reduce_scatter | solution.py:105
  106.9 12.7 %collective-permute-start.1 = (bf16[256,1024]{1,0:T(8,128)(2,1)S(1)}, bf16[256,1024]{1,0:T(8,128)(2,1)S(1)}, u32[]{:S(2)}, u32[]{:S(2)}) collective-permute-start(bf16[256,1024]{1,0:T(8,128)(2,1)S(1)} %get-tuple-element.11), channel_id=1, source_target_pairs={{0,1},{1,0},{2,3},{3,2},{4,5},{5,4},{6,7},{7,6},{8,9},{9,8},{10,11... | collective-permute-start | bytes 1572872 | tf_op jit(solution)/shard_map/ppermute | solution.py:85
  237.0 4.9 %all-to-all-start.2 = ((bf16[2,16,2560]{2,1,0:T(8,128)(2,1)}), bf16[2,16,2560]{2,1,0:T(8,128)(2,1)S(1)}, u32[]{:S(2)}, u32[]{:S(2)}) async-start(bf16[2,16,2560]{2,1,0:T(8,128)(2,1)} %bitcast.94), calls=%async_computation.4 | async-start | bytes 327680 | tf_op jit(solution)/shard_map/all_to_all | solution.py:29
Sparse Core Ops, SparseCore 0:
  14.4 44.5 all-gather.2
  61.7 40.6 all-gather.4
  105.8 63.8 reduce-scatter.2
  173.0 63.9 reduce-scatter.4

commit v2 on v1

--- a/solution.py
+++ b/solution.py
@@ -1,6 +1,10 @@
+import functools
+
 import jax
 import jax.numpy as jnp
 from jax import lax
+from jax.experimental import pallas as pl
+from jax.experimental.pallas import tpu as pltpu
 from jax.sharding import PartitionSpec as P
 
 HIGHEST = lax.Precision.HIGHEST
@@ -39,6 +43,283 @@
 
 def share_fold(shares, step_fn, start_value):
     return step_fn(start_value, lax.all_gather(shares, "dp", axis=2, tiled=True), jnp.int32(0))
+
+
+MESH = pl.DeviceIdType.MESH
+LANES = 2
+
+
+def greet(groups, me, lines):
+    my_group = lax.axis_index("group")
+    line = me // LANES
+    barrier = pltpu.get_barrier_semaphore()
+
+    def hello(where):
+        pl.semaphore_signal(barrier, inc=1, device_id=where, device_id_type=MESH)
+
+    for step in range(1, groups):
+        hello({"group": lax.rem(my_group + step, groups)})
+    hello({"expert": line * LANES + 1 - lax.rem(me, LANES)})
+
+    @pl.when(line < lines - 1)
+    def _():
+        hello({"expert": me + LANES})
+
+    @pl.when(line > 0)
+    def _():
+        hello({"expert": me - LANES})
+
+    ends = (line < lines - 1).astype(jnp.int32) + (line > 0).astype(jnp.int32)
+    pl.semaphore_wait(barrier, groups + ends)
+
+
+def gather_kernel(groups, members, leaving, out, own_sem, pair_send, pair_recv, send, recv):
+    lines = members // LANES
+    my_group = lax.axis_index("group")
+    me = lax.axis_index("expert")
+    line, lane = me // LANES, lax.rem(me, LANES)
+    beside = line * LANES + 1 - lane
+    greet(groups, me, lines)
+
+    def pair_copy(step):
+        other = lax.rem(my_group + step, groups)
+        return pltpu.make_async_remote_copy(
+            src_ref=leaving.at[other],
+            dst_ref=out.at[me, my_group],
+            send_sem=pair_send.at[step],
+            recv_sem=pair_recv.at[step],
+            device_id={"group": other},
+            device_id_type=MESH,
+        )
+
+    def pair_wait(step):
+        source = lax.rem(my_group + groups - step, groups)
+        pltpu.make_async_remote_copy(
+            src_ref=leaving.at[source],
+            dst_ref=out.at[me, source],
+            send_sem=pair_send.at[step],
+            recv_sem=pair_recv.at[step],
+            device_id={"group": source},
+            device_id_type=MESH,
+        ).wait_recv()
+
+    def hop(way, block, target):
+        return pltpu.make_async_remote_copy(
+            src_ref=out.at[block],
+            dst_ref=out.at[block],
+            send_sem=send.at[way, block],
+            recv_sem=recv.at[block],
+            device_id={"expert": target},
+            device_id_type=MESH,
+        )
+
+    for step in range(1, groups):
+        pair_copy(step).start()
+    own = pltpu.make_async_copy(leaving.at[my_group], out.at[me, my_group], own_sem)
+    own.start()
+    own.wait()
+    for step in range(1, groups):
+        pair_wait(step)
+
+    def visit(act_up, act_down, act_side, arrive):
+        hop_up, hop_down, hop_side = act_up, act_down, act_side
+        hop_side(me)
+        pl.when(line < lines - 1)(lambda: hop_up(me))
+        pl.when(line > 0)(lambda: hop_down(me))
+        for reach in range(1, lines):
+            @pl.when(line - reach >= 0)
+            def _():
+                block = me - reach * LANES
+                arrive(block)
+                pl.when(line < lines - 1)(lambda: hop_up(block))
+                hop_side(block)
+
+            @pl.when(line + reach <= lines - 1)
+            def _():
+                block = me + reach * LANES
+                arrive(block)
+                pl.when(line > 0)(lambda: hop_down(block))
+                hop_side(block)
+
+    visit(
+        lambda block: hop(0, block, me + LANES).start(),
+        lambda block: hop(1, block, me - LANES).start(),
+        lambda block: hop(2, block, beside).start(),
+        lambda block: hop(0, block, beside).wait_recv(),
+    )
+    for place in range(lines):
+        hop(2, place * LANES + 1 - lane, beside).wait_recv()
+    visit(
+        lambda block: hop(0, block, me + LANES).wait_send(),
+        lambda block: hop(1, block, me - LANES).wait_send(),
+        lambda block: hop(2, block, beside).wait_send(),
+        lambda block: None,
+    )
+    for step in range(1, groups):
+        pair_copy(step).wait_send()
+
+
+def reduce_kernel(
+    groups, members, parts, home, side, up, down, passing, total,
+    pair_send, pair_recv, side_send, side_recv, line_send, up_recv, down_recv,
+):
+    lines = members // LANES
+    my_group = lax.axis_index("group")
+    me = lax.axis_index("expert")
+    line, lane = me // LANES, lax.rem(me, LANES)
+    beside = line * LANES + 1 - lane
+    greet(groups, me, lines)
+
+    def side_copy(place):
+        return pltpu.make_async_remote_copy(
+            src_ref=parts.at[place * LANES + 1 - lane],
+            dst_ref=side.at[place],
+            send_sem=side_send.at[place],
+            recv_sem=side_recv.at[place],
+            device_id={"expert": beside},
+            device_id_type=MESH,
+        )
+
+    def line_copy(land, recv, place, target):
+        return pltpu.make_async_remote_copy(
+            src_ref=passing.at[place],
+            dst_ref=land.at[place],
+            send_sem=line_send.at[place],
+            recv_sem=recv.at[place],
+            device_id={"expert": target},
+            device_id_type=MESH,
+        )
+
+    def up_copy(place):
+        return line_copy(up, up_recv, place, me + LANES)
+
+    def down_copy(place):
+        return line_copy(down, down_recv, place, me - LANES)
+
+    def far_first(above, below):
+        for reach in range(lines - 1, 0, -1):
+            pl.when(line + reach <= lines - 1)(functools.partial(above, line + reach))
+            pl.when(line - reach >= 0)(functools.partial(below, line - reach))
+
+    def begin(place):
+        side_copy(place).start()
+
+    far_first(begin, begin)
+    begin(line)
+
+    def pair_sum(place):
+        side_copy(place).wait_recv()
+        mine = parts[place * LANES + lane].astype(jnp.float32)
+        return mine + side[place].astype(jnp.float32)
+
+    def pass_on(place, land, copy_of, has_before):
+        passing[place] = pair_sum(place).astype(passing.dtype)
+
+        @pl.when(has_before)
+        def _():
+            copy_of(place).wait_recv()
+            both = passing_f32(place) + land[place].astype(jnp.float32)
+            passing[place] = both.astype(passing.dtype)
+
+        copy_of(place).start()
+
+    def passing_f32(place):
+        mine = parts[place * LANES + lane].astype(jnp.float32)
+        return mine + side[place].astype(jnp.float32)
+
+    far_first(
+        lambda place: pass_on(place, up, up_copy, line > 0),
+        lambda place: pass_on(place, down, down_copy, line < lines - 1),
+    )
+    total[...] = pair_sum(line)
+
+    @pl.when(line > 0)
+    def _():
+        up_copy(line).wait_recv()
+        total[...] += up[line].astype(jnp.float32)
+
+    @pl.when(line < lines - 1)
+    def _():
+        down_copy(line).wait_recv()
+        total[...] += down[line].astype(jnp.float32)
+
+    passing[line] = total[...].astype(passing.dtype)
+
+    def pair_copy(step):
+        other = lax.rem(my_group + step, groups)
+        return pltpu.make_async_remote_copy(
+            src_ref=passing.at[line, other],
+            dst_ref=home.at[my_group],
+            send_sem=pair_send.at[step],
+            recv_sem=pair_recv.at[step],
+            device_id={"group": other},
+            device_id_type=MESH,
+        )
+
+    for step in range(1, groups):
+        pair_copy(step).start()
+    home[my_group] = passing[line, my_group]
+    for step in range(1, groups):
+        source = lax.rem(my_group + groups - step, groups)
+        pltpu.make_async_remote_copy(
+            src_ref=passing.at[line, source],
+            dst_ref=home.at[source],
+            send_sem=pair_send.at[step],
+            recv_sem=pair_recv.at[step],
+            device_id={"group": source},
+            device_id_type=MESH,
+        ).wait_recv()
+        pair_copy(step).wait_send()
+    far_first(
+        lambda place: up_copy(place).wait_send(),
+        lambda place: down_copy(place).wait_send(),
+    )
+    for place in range(lines):
+        side_copy(place).wait_send()
+
+
+def comm_cost(array, members):
+    return pl.CostEstimate(
+        flops=0, bytes_accessed=32 * members * array.size * 2 // 2, transcendentals=0
+    )
+
+
+def gather_rows(leaving, members):
+    groups, visitors, features = leaving.shape
+    dma = pltpu.SemaphoreType.DMA
+    return pl.pallas_call(
+        functools.partial(gather_kernel, groups, members),
+        out_shape=jax.ShapeDtypeStruct((members, *leaving.shape), leaving.dtype),
+        in_specs=[pl.BlockSpec(memory_space=pltpu.VMEM)],
+        out_specs=pl.BlockSpec(memory_space=pltpu.VMEM),
+        scratch_shapes=[
+            dma(()), dma((groups,)), dma((groups,)), dma((3, members)), dma((members,)),
+        ],
+        compiler_params=pltpu.CompilerParams(collective_id=0, has_side_effects=True),
+        cost_estimate=comm_cost(leaving, members),
+        name="gather_rows",
+    )(leaving)
+
+
+def reduce_rows(parts, groups, members):
+    block = (groups, parts.shape[0] // (groups * members), parts.shape[1])
+    lines = members // LANES
+    dma = pltpu.SemaphoreType.DMA
+    slots = pltpu.VMEM((lines, *block), parts.dtype)
+    return pl.pallas_call(
+        functools.partial(reduce_kernel, groups, members),
+        out_shape=jax.ShapeDtypeStruct(block, parts.dtype),
+        in_specs=[pl.BlockSpec(memory_space=pltpu.VMEM)],
+        out_specs=pl.BlockSpec(memory_space=pltpu.VMEM),
+        scratch_shapes=[
+            slots, slots, slots, slots, pltpu.VMEM(block, jnp.float32),
+            dma((groups,)), dma((groups,)), dma((lines,)), dma((lines,)),
+            dma((lines,)), dma((lines,)), dma((lines,)),
+        ],
+        compiler_params=pltpu.CompilerParams(collective_id=1, has_side_effects=True),
+        cost_estimate=comm_cost(parts, 1),
+        name="reduce_rows",
+    )(parts.reshape(members, *block))
 
 
 def dense_device(tokens, grad_out, expert_ids, gate_score, w_gate_up, w_down):
@@ -68,13 +349,14 @@
     gate_weights = w_gate_up[0]
     down_weights = w_down[0]
 
-    both = jnp.concatenate([tokens, grad_out], axis=1)
-    leaving = jnp.einsum(
-        "gst,tf->gsf", leave_table, both, preferred_element_type=jnp.float32
-    ).astype(jnp.bfloat16)
-    arrived = across(leaving).reshape(arrivals, 2 * features)
-    rows_in = lax.all_gather(arrived[:, :features], "expert", axis=0, tiled=True)
-    rows_grad = lax.all_gather(arrived[:, features:], "expert", axis=0, tiled=True)
+    def dispatch(values):
+        leaving = jnp.einsum(
+            "gst,tf->gsf", leave_table, values, preferred_element_type=jnp.float32
+        ).astype(jnp.bfloat16)
+        return gather_rows(leaving, members).reshape(expert_rows, features)
+
+    rows_in = dispatch(tokens)
+    rows_grad = dispatch(grad_out)
 
     swap = [(i, (i + 1) % shares) for i in range(shares)]
 
@@ -101,16 +383,14 @@
     grad_part = jnp.einsum(
         "rkh,fkh->rf", pre_grad, gate_weights, preferred_element_type=jnp.float32
     ).astype(jnp.bfloat16)
-    out_sum = lax.psum_scatter(out_part, "expert", scatter_dimension=0, tiled=True)
-    grad_total = lax.psum_scatter(grad_part, "expert", scatter_dimension=0, tiled=True)
-
-    def give_back(summed):
-        home = across(summed.reshape(groups, visitors, features))
+
+    def give_back(parts):
+        home = reduce_rows(parts, groups, members)
         return jnp.einsum(
             "gst,gsf->tf", leave_table, home, preferred_element_type=jnp.float32
         ).astype(jnp.bfloat16)
 
-    return (give_back(out_sum), give_back(grad_total))
+    return (give_back(out_part), give_back(grad_part))
 
 
 def on_device(tokens, grad_out, expert_ids, gate_score, w_gate_up, w_down):
@@ -208,7 +488,8 @@
 
 
 def per_device(tokens, grad_out, expert_ids, gate_score, w_gate_up, w_down):
-    dense = expert_ids.shape[1] == lax.axis_size("expert")
+    members = lax.axis_size("expert")
+    dense = expert_ids.shape[1] == members and members % LANES == 0
     plan = dense_device if dense else on_device
     return plan(tokens, grad_out, expert_ids, gate_score, w_gate_up, w_down)
 

time: 250 us -> 144 us (0.58)
  waiting for transfers between devices: 184 us -> 0.01 us
  Pallas kernels: 0 us -> 100 us
  between operations: 13.8 us -> 0.77 us
  blocking collectives: 8.89 us -> 0 us
  starting transfers between devices: 6.58 us -> 2.02 us
  matrix products: 30.4 us -> 33.7 us
    reduce_scatter x2 -> x0, waiting for transfers between devices: 103 us -> none  [the longest x1 62.3 us: dense_device(): lax.psum_scatter(grad_part, 'expert', scatter_dimension=0, tiled=True)]
    pallas_call x0 -> x4, Pallas kernels: none -> 100 us  [the longest x2 53.1 us: gather_rows(): pl.pallas_call(functools.partial(gather_kernel, groups, members), out_sha...]
    all_gather x2 -> x0, waiting for transfers between devices: 47.1 us -> none  [the longest x1 43.9 us: dense_device(): lax.all_gather(arrived[:, :features], 'expert', axis=0, tiled=True)]
    ppermute x2, waiting for transfers between devices: 32.9 us -> 0.01 us  [dp_sum(): moving = lax.ppermute(moving, 'dp', swap)]
    all_to_all x2 -> x0, blocking collectives: 8.89 us -> none  [across(): lax.all_to_all(blocks, 'group', split_axis=0, concat_axis=0, tiled=True)]
    all_to_all x1 -> x0, starting transfers between devices: 3.42 us -> none  [across(): lax.all_to_all(blocks, 'group', split_axis=0, concat_axis=0, tiled=True)]
  transfers between devices with their start and end apart: 7 -> 2, of which waited for: 7 -> 0; matrix products, arithmetic and copies ran while one was open for 13% -> 11% of each run, Pallas kernels for 0% -> 34%
where the time goes in v2:
time: 144 us; the launch traced here: 143 us
  Pallas kernels  100 us (69%)
  matrix products  33.7 us (23%)
  other arithmetic  4.49 us (3%)
  local copies, waits for them, and re-layouts  2.12 us (1%)
  starting transfers between devices  2.02 us (1%)
    pallas_call x2, Pallas kernels, gather_rows(): pl.pallas_call(functools.partial(gather_kernel, groups, members), out_sha...  53.1 us
    pallas_call x2, Pallas kernels, reduce_rows(): pl.pallas_call(functools.partial(reduce_kernel, groups, members), out_sha...  47 us
    dot_general x1, matrix products, dense_device(): jnp.einsum('rf,fkh->rkh', rows_in, gate_weights, preferred_element_type=j...  9.46 us
    dot_general x1, matrix products, dense_device(): jnp.einsum('rkh,fkh->rf', pre_grad, gate_weights, preferred_element_type=...  8.58 us
    dot_general x1, matrix products, dense_device(): jnp.einsum('rf,hf->rh', rows_grad, down_weights, preferred_element_type=j...  5.24 us
    dot_general x1, matrix products, dense_device(): jnp.dot(hidden, down_weights, preferred_element_type=jnp.float32)  5.11 us
    dot_general x2, matrix products, give_back(): jnp.einsum('gst,gsf->tf', leave_table, home, preferred_element_type=jnp.f...  3.62 us
  transfers between devices with their start and end apart: 2, of which 0 were waited for; matrix products, arithmetic and copies ran while one was open for 11% of the time, Pallas kernels for 34%

profile of v2, /device:TPU:0, one launch (start us, length us, event | category | flops | bytes accessed | tf_op | source)
XLA Modules:
  0.0 143.2 jit_solution(5053188420369460675)
XLA Ops:
  0.6 0.0 copy-start
  0.6 0.8 slice_reduce_fusion
  1.4 0.1 squeeze.19
  1.5 0.1 fusion.41
  1.6 0.1 reduce_window_sum.22
  1.7 0.1 copy.14
  1.8 0.0 copy-done
  1.8 0.9 convolution_convert_fusion.1.leaving
  2.6 27.5 %gather_rows.2 = bf16[8,2,16,2560]{3,2,1,0:T(8,128)(2,1)} custom-call(bf16[2,16,2560]{2,1,0:T(8,128)(2,1)} %convolution_convert_fusion.1.leaving), custom_call_target="tpu_custom_call" | custom-call | bytes 20971520 | tf_op jit(solution)/shard_map/gather_rows/pallas_call | solution.py:290
  30.1 0.0 copy-start.2
  30.1 9.5 %fusion.57 = (bf16[256,2,1024]{2,0,1:T(8,128)(2,1)}, f32[256,2,1024]{2,0,1:T(8,128)}) fusion(bf16[256,2560,1]{1,0,2:T(8,128)(2,1)} %bitcast.94, bf16[2560,2,1024]{2,1,0:T(2,128)(2,1)} %bitcast.99), kind=kOutput, calls=%fused_computation.78 | convolution fusion | flops 2684878848 | bytes 14942208 | tf_op jit(solution)/shard_map/rf,fkh->rkh/dot_general | solution.py:372
  39.6 1.5 %collective-permute-start = (bf16[256,2,1024]{2,0,1:T(8,128)(2,1)}, bf16[256,2,1024]{2,0,1:T(8,128)(2,1)S(1)}, u32[]{:S(2)}, u32[]{:S(2)}) collective-permute-start(bf16[256,2,1024]{2,0,1:T(8,128)(2,1)} %get-tuple-element.7), channel_id=1, source_target_pairs={{0,1},{1,0},{2,3},{3,2},{4,5},{5,4},{6,7},{7,6},{8,9},{9,8},{10,11... | collective-permute-start | bytes 3145736 | tf_op jit(solution)/shard_map/ppermute | solution.py:367
  41.0 0.0 copy-done.2
  41.1 0.8 convolution_convert_fusion.leaving
  41.9 25.6 %gather_rows.3 = bf16[8,2,16,2560]{3,2,1,0:T(8,128)(2,1)} custom-call(bf16[2,16,2560]{2,1,0:T(8,128)(2,1)} %convolution_convert_fusion.leaving), custom_call_target="tpu_custom_call" | custom-call | bytes 20971520 | tf_op jit(solution)/shard_map/gather_rows/pallas_call | solution.py:290
  67.5 0.0 copy-start.3
  67.5 0.0 copy-start.4
  67.5 5.2 %fusion.58 = (bf16[256,1024]{1,0:T(8,128)(2,1)}, f32[256,1024]{1,0:T(8,128)S(1)}) fusion(bf16[256,2560]{1,0:T(8,128)(2,1)} %bitcast.95, bf16[1,1024,2560]{2,1,0:T(8,128)(2,1)} %param.11), kind=kOutput, calls=%fused_computation.79 | convolution fusion | flops 1342439424 | bytes 8126464 | tf_op jit(solution)/shard_map/rf,hf->rh/dot_general | solution.py:375
  72.8 0.5 collective-permute-start.1
  73.3 0.0 copy-done.3
  73.3 0.0 copy-done.4
  73.4 0.1 mul.69
  73.5 0.4 reduce_window_sum.23
  73.8 0.1 select_reduce_fusion
  74.0 0.1 mul.72
  74.1 0.0 collective-permute-done
  74.1 0.0 copy-start.1
  74.1 1.0 copy-done.1
  75.0 2.1 %convert_add_fusion = f32[256,2,1024]{2,0,1:T(8,128)S(1)} fusion(f32[256,2,1024]{2,0,1:T(8,128)} %get-tuple-element.8, bf16[256,2,1024]{2,0,1:T(8,128)(2,1)} %copy-done.1), kind=kLoop, calls=%fused_computation.18 | loop fusion | flops 1048576 | bytes 5242880 | tf_op jit(solution)/shard_map/add | solution.py:368
  77.2 5.1 %fusion.17 = bf16[256,2560]{1,0:T(8,128)(2,1)} fusion(bf16[1,1024,2560]{2,1,0:T(8,128)(2,1)} %param.11, f32[256]{0:T(256)S(1)} %mul.72, f32[256,2,1024]{2,0,1:T(8,128)S(1)} %convert_add_fusion), kind=kOutput, calls=%fused_computation.11 | convolution fusion | flops 1345060864 | bytes 8651776 | tf_op jit(solution)/shard_map/dot_general | solution.py:380
  82.3 23.5 %reduce_rows.2 = bf16[2,16,2560]{2,1,0:T(8,128)(2,1)} custom-call(bf16[8,2,16,2560]{3,2,1,0:T(8,128)(2,1)} %bitcast.97), custom_call_target="tpu_custom_call" | custom-call | bytes 20971520 | tf_op jit(solution)/shard_map/reduce_rows/pallas_call | solution.py:309
  105.8 1.8 %fusion.20 = bf16[32,2560]{1,0:T(8,128)(2,1)} fusion(bf16[2,16,2560]{2,1,0:T(8,128)(2,1)} %reduce_rows.2, s32[2,32]{1,0:T(2,128)S(1)} %copy.14, pred[2,32]{1,0:T(4,128)(4,1)S(1)} %iota_compare_fusion.3), kind=kOutput, calls=%fused_computation.14 | convolution fusion | flops 5328896 | bytes 328000 | tf_op jit(solution)/shard_map/gst,gsf->tf/dot_general | solution.py:389
  107.6 0.0 collective-permute-done.1
  107.6 1.6 %fusion.36 = (bf16[256,1,1024]{2,0,1:T(8,128)(2,1)S(1)}, bf16[256,1,1024]{2,0,1:T(8,128)(2,1)S(1)}) fusion(f32[256,2,1024]{2,0,1:T(8,128)S(1)} %convert_add_fusion, f32[256]{0:T(256)S(1)} %mul.72, f32[256,1024]{1,0:T(8,128)S(1)} %get-tuple-element.10, bf16[256,1024]{1,0:T(8,128)(2,1)} %collective-permute-done.1), kind=kLoop, calls=%fused_computation.39 | loop fusion | flops 4194304 | bytes 4719616 | tf_op jit(solution)/shard_map/stack | solution.py:29
  109.3 8.6 %fusion.14 = bf16[256,2560]{1,0:T(8,128)(2,1)} fusion(bf16[2560,2,1024]{2,1,0:T(2,128)(2,1)} %bitcast.100, bf16[256,1,1024]{2,0,1:T(8,128)(2,1)S(1)} %get-tuple-element.6, bf16[256,1,1024]{2,0,1:T(8,128)(2,1)S(1)} %get-tuple-element.5), kind=kOutput, calls=%fused_computation.10 | convolution fusion | flops 2685534208 | bytes 12845056 | tf_op jit(solution)/shard_map/rkh,fkh->rf/dot_general | solution.py:383
  117.9 23.5 %reduce_rows.3 = bf16[2,16,2560]{2,1,0:T(8,128)(2,1)} custom-call(bf16[8,2,16,2560]{3,2,1,0:T(8,128)(2,1)} %bitcast.96), custom_call_target="tpu_custom_call" | custom-call | bytes 20971520 | tf_op jit(solution)/shard_map/reduce_rows/pallas_call | solution.py:309
  141.4 1.8 %fusion.21 = bf16[32,2560]{1,0:T(8,128)(2,1)} fusion(bf16[2,16,2560]{2,1,0:T(8,128)(2,1)} %reduce_rows.3, s32[2,32]{1,0:T(2,128)S(1)} %copy.14, pred[2,32]{1,0:T(4,128)(4,1)S(1)} %iota_compare_fusion.3), kind=kOutput, calls=%fused_computation.15 | convolution fusion | flops 5328896 | bytes 328000 | tf_op jit(solution)/shard_map/gst,gsf->tf/dot_general | solution.py:389
  (8 shorter events, 0.1 us)
Async XLA Ops:
  0.6 1.1 copy-start
  30.1 11.0 %copy-start.2 = (bf16[32,2560]{1,0:T(8,128)(2,1)S(1)}, bf16[32,2560]{1,0:T(8,128)(2,1)}, u32[]{:S(2)}) copy-start(bf16[32,2560]{1,0:T(8,128)(2,1)} %param.7) | copy-start | bytes 491524
  39.6 34.5 %collective-permute-start = (bf16[256,2,1024]{2,0,1:T(8,128)(2,1)}, bf16[256,2,1024]{2,0,1:T(8,128)(2,1)S(1)}, u32[]{:S(2)}, u32[]{:S(2)}) collective-permute-start(bf16[256,2,1024]{2,0,1:T(8,128)(2,1)} %get-tuple-element.7), channel_id=1, source_target_pairs={{0,1},{1,0},{2,3},{3,2},{4,5},{5,4},{6,7},{7,6},{8,9},{9,8},{10,11... | collective-permute-start | bytes 3145736 | tf_op jit(solution)/shard_map/ppermute | solution.py:367
  67.5 5.8 %copy-start.3 = (f32[512,8]{0,1:T(8,128)S(1)}, f32[512,8]{0,1:T(8,128)}, u32[]{:S(2)}) copy-start(f32[512,8]{0,1:T(8,128)} %param.9) | copy-start | bytes 49156
  67.5 5.8 %copy-start.4 = (s32[512,8]{0,1:T(8,128)S(1)}, s32[512,8]{0,1:T(8,128)}, u32[]{:S(2)}) copy-start(s32[512,8]{0,1:T(8,128)} %param.8) | copy-start | bytes 49156
  72.8 34.9 %collective-permute-start.1 = (bf16[256,1024]{1,0:T(8,128)(2,1)}, bf16[256,1024]{1,0:T(8,128)(2,1)}, u32[]{:S(2)}, u32[]{:S(2)}) collective-permute-start(bf16[256,1024]{1,0:T(8,128)(2,1)} %get-tuple-element.9), channel_id=1, source_target_pairs={{0,1},{1,0},{2,3},{3,2},{4,5},{5,4},{6,7},{7,6},{8,9},{9,8},{10,11... | collective-permute-start | bytes 1572872 | tf_op jit(solution)/shard_map/ppermute | solution.py:367
  74.1 1.0 copy-start.1

commit v3 on v2

--- a/solution.py
+++ b/solution.py
@@ -103,58 +103,74 @@
             device_id_type=MESH,
         ).wait_recv()
 
-    def hop(way, block, target):
+    def hop(way, block, piece, target):
         return pltpu.make_async_remote_copy(
-            src_ref=out.at[block],
-            dst_ref=out.at[block],
-            send_sem=send.at[way, block],
-            recv_sem=recv.at[block],
+            src_ref=out.at[block, piece],
+            dst_ref=out.at[block, piece],
+            send_sem=send.at[way, block, piece],
+            recv_sem=recv.at[block, piece],
             device_id={"expert": target},
             device_id_type=MESH,
         )
+
+    def hop_up(block, piece):
+        return hop(0, block, piece, me + LANES)
+
+    def hop_down(block, piece):
+        return hop(1, block, piece, me - LANES)
+
+    def hop_side(block, piece):
+        return hop(2, block, piece, beside)
 
     for step in range(1, groups):
         pair_copy(step).start()
     own = pltpu.make_async_copy(leaving.at[my_group], out.at[me, my_group], own_sem)
     own.start()
     own.wait()
-    for step in range(1, groups):
-        pair_wait(step)
-
-    def visit(act_up, act_down, act_side, arrive):
-        hop_up, hop_down, hop_side = act_up, act_down, act_side
-        hop_side(me)
-        pl.when(line < lines - 1)(lambda: hop_up(me))
-        pl.when(line > 0)(lambda: hop_down(me))
-        for reach in range(1, lines):
-            @pl.when(line - reach >= 0)
-            def _():
-                block = me - reach * LANES
-                arrive(block)
-                pl.when(line < lines - 1)(lambda: hop_up(block))
-                hop_side(block)
-
-            @pl.when(line + reach <= lines - 1)
-            def _():
-                block = me + reach * LANES
-                arrive(block)
-                pl.when(line > 0)(lambda: hop_down(block))
-                hop_side(block)
-
-    visit(
-        lambda block: hop(0, block, me + LANES).start(),
-        lambda block: hop(1, block, me - LANES).start(),
-        lambda block: hop(2, block, beside).start(),
-        lambda block: hop(0, block, beside).wait_recv(),
-    )
+
+    def visit(reach, act, arrive):
+        for step in range(groups):
+            def above(block, piece):
+                arrive(block, piece)
+                pl.when(line > 0)(lambda: act(hop_down(block, piece)))
+                act(hop_side(block, piece))
+
+            def below(block, piece):
+                arrive(block, piece)
+                pl.when(line < lines - 1)(lambda: act(hop_up(block, piece)))
+                act(hop_side(block, piece))
+
+            piece = lax.rem(my_group + groups - step, groups)
+            pl.when(line - reach >= 0)(functools.partial(below, me - reach * LANES, piece))
+            pl.when(line + reach <= lines - 1)(
+                functools.partial(above, me + reach * LANES, piece)
+            )
+
+    def visit_own(step, act):
+        piece = lax.rem(my_group + groups - step, groups)
+        act(hop_side(me, piece))
+        pl.when(line < lines - 1)(lambda: act(hop_up(me, piece)))
+        pl.when(line > 0)(lambda: act(hop_down(me, piece)))
+
+    def begin(copy):
+        copy.start()
+
+    def sent(copy):
+        copy.wait_send()
+
+    for step in range(groups):
+        if step:
+            pair_wait(step)
+        visit_own(step, begin)
+    for reach in range(1, lines):
+        visit(reach, begin, lambda block, piece: hop_side(block, piece).wait_recv())
     for place in range(lines):
-        hop(2, place * LANES + 1 - lane, beside).wait_recv()
-    visit(
-        lambda block: hop(0, block, me + LANES).wait_send(),
-        lambda block: hop(1, block, me - LANES).wait_send(),
-        lambda block: hop(2, block, beside).wait_send(),
-        lambda block: None,
-    )
+        for piece in range(groups):
+            hop_side(place * LANES + 1 - lane, piece).wait_recv()
+    for step in range(groups):
+        visit_own(step, sent)
+    for reach in range(1, lines):
+        visit(reach, sent, lambda block, piece: None)
     for step in range(1, groups):
         pair_copy(step).wait_send()
 
@@ -170,80 +186,71 @@
     beside = line * LANES + 1 - lane
     greet(groups, me, lines)
 
-    def side_copy(place):
+    def side_copy(place, piece):
         return pltpu.make_async_remote_copy(
-            src_ref=parts.at[place * LANES + 1 - lane],
-            dst_ref=side.at[place],
-            send_sem=side_send.at[place],
-            recv_sem=side_recv.at[place],
+            src_ref=parts.at[place * LANES + 1 - lane, piece],
+            dst_ref=side.at[place, piece],
+            send_sem=side_send.at[place, piece],
+            recv_sem=side_recv.at[place, piece],
             device_id={"expert": beside},
             device_id_type=MESH,
         )
 
-    def line_copy(land, recv, place, target):
+    def line_copy(land, recv, place, piece, target):
         return pltpu.make_async_remote_copy(
-            src_ref=passing.at[place],
-            dst_ref=land.at[place],
-            send_sem=line_send.at[place],
-            recv_sem=recv.at[place],
+            src_ref=passing.at[place, piece],
+            dst_ref=land.at[place, piece],
+            send_sem=line_send.at[place, piece],
+            recv_sem=recv.at[place, piece],
             device_id={"expert": target},
             device_id_type=MESH,
         )
 
-    def up_copy(place):
-        return line_copy(up, up_recv, place, me + LANES)
-
-    def down_copy(place):
-        return line_copy(down, down_recv, place, me - LANES)
+    def up_copy(place, piece):
+        return line_copy(up, up_recv, place, piece, me + LANES)
+
+    def down_copy(place, piece):
+        return line_copy(down, down_recv, place, piece, me - LANES)
 
     def far_first(above, below):
         for reach in range(lines - 1, 0, -1):
-            pl.when(line + reach <= lines - 1)(functools.partial(above, line + reach))
-            pl.when(line - reach >= 0)(functools.partial(below, line - reach))
-
-    def begin(place):
-        side_copy(place).start()
+            for step in range(groups):
+                piece = lax.rem(my_group + 1 + step, groups)
+                pl.when(line + reach <= lines - 1)(
+                    functools.partial(above, line + reach, piece)
+                )
+                pl.when(line - reach >= 0)(functools.partial(below, line - reach, piece))
+
+    def begin(place, piece):
+        side_copy(place, piece).start()
 
     far_first(begin, begin)
-    begin(line)
-
-    def pair_sum(place):
-        side_copy(place).wait_recv()
-        mine = parts[place * LANES + lane].astype(jnp.float32)
-        return mine + side[place].astype(jnp.float32)
-
-    def pass_on(place, land, copy_of, has_before):
-        passing[place] = pair_sum(place).astype(passing.dtype)
+    for step in range(groups):
+        begin(line, lax.rem(my_group + 1 + step, groups))
+
+    def pair_sum(place, piece):
+        mine = parts[place * LANES + lane, piece].astype(jnp.float32)
+        return mine + side[place, piece].astype(jnp.float32)
+
+    def pass_on(land, copy_of, has_before, place, piece):
+        side_copy(place, piece).wait_recv()
 
         @pl.when(has_before)
         def _():
-            copy_of(place).wait_recv()
-            both = passing_f32(place) + land[place].astype(jnp.float32)
-            passing[place] = both.astype(passing.dtype)
-
-        copy_of(place).start()
-
-    def passing_f32(place):
-        mine = parts[place * LANES + lane].astype(jnp.float32)
-        return mine + side[place].astype(jnp.float32)
+            copy_of(place, piece).wait_recv()
+            both = pair_sum(place, piece) + land[place, piece].astype(jnp.float32)
+            passing[place, piece] = both.astype(passing.dtype)
+
+        @pl.when(jnp.logical_not(has_before))
+        def _():
+            passing[place, piece] = pair_sum(place, piece).astype(passing.dtype)
+
+        copy_of(place, piece).start()
 
     far_first(
-        lambda place: pass_on(place, up, up_copy, line > 0),
-        lambda place: pass_on(place, down, down_copy, line < lines - 1),
-    )
-    total[...] = pair_sum(line)
-
-    @pl.when(line > 0)
-    def _():
-        up_copy(line).wait_recv()
-        total[...] += up[line].astype(jnp.float32)
-
-    @pl.when(line < lines - 1)
-    def _():
-        down_copy(line).wait_recv()
-        total[...] += down[line].astype(jnp.float32)
-
-    passing[line] = total[...].astype(passing.dtype)
+        functools.partial(pass_on, up, up_copy, line > 0),
+        functools.partial(pass_on, down, down_copy, line < lines - 1),
+    )
 
     def pair_copy(step):
         other = lax.rem(my_group + step, groups)
@@ -256,9 +263,26 @@
             device_id_type=MESH,
         )
 
-    for step in range(1, groups):
-        pair_copy(step).start()
-    home[my_group] = passing[line, my_group]
+    for step in range(1, groups + 1):
+        piece = lax.rem(my_group + step, groups)
+        side_copy(line, piece).wait_recv()
+        total[...] = pair_sum(line, piece)
+
+        @pl.when(line > 0)
+        def _():
+            up_copy(line, piece).wait_recv()
+            total[...] += up[line, piece].astype(jnp.float32)
+
+        @pl.when(line < lines - 1)
+        def _():
+            down_copy(line, piece).wait_recv()
+            total[...] += down[line, piece].astype(jnp.float32)
+
+        if step < groups:
+            passing[line, piece] = total[...].astype(passing.dtype)
+            pair_copy(step).start()
+        else:
+            home[my_group] = total[...].astype(home.dtype)
     for step in range(1, groups):
         source = lax.rem(my_group + groups - step, groups)
         pltpu.make_async_remote_copy(
@@ -271,11 +295,12 @@
         ).wait_recv()
         pair_copy(step).wait_send()
     far_first(
-        lambda place: up_copy(place).wait_send(),
-        lambda place: down_copy(place).wait_send(),
+        lambda place, piece: up_copy(place, piece).wait_send(),
+        lambda place, piece: down_copy(place, piece).wait_send(),
     )
     for place in range(lines):
-        side_copy(place).wait_send()
+        for piece in range(groups):
+            side_copy(place, piece).wait_send()
 
 
 def comm_cost(array, members):
@@ -293,9 +318,13 @@
         in_specs=[pl.BlockSpec(memory_space=pltpu.VMEM)],
         out_specs=pl.BlockSpec(memory_space=pltpu.VMEM),
         scratch_shapes=[
-            dma(()), dma((groups,)), dma((groups,)), dma((3, members)), dma((members,)),
+            dma(()),
+            dma((groups,)), dma((groups,)),
+            dma((3, members, groups)), dma((members, groups)),
         ],
-        compiler_params=pltpu.CompilerParams(collective_id=0, has_side_effects=True),
+        compiler_params=pltpu.CompilerParams(
+            collective_id=0, has_side_effects=True, vmem_limit_bytes=8 << 20
+        ),
         cost_estimate=comm_cost(leaving, members),
         name="gather_rows",
     )(leaving)
@@ -312,11 +341,12 @@
         in_specs=[pl.BlockSpec(memory_space=pltpu.VMEM)],
         out_specs=pl.BlockSpec(memory_space=pltpu.VMEM),
         scratch_shapes=[
-            slots, slots, slots, slots, pltpu.VMEM(block, jnp.float32),
-            dma((groups,)), dma((groups,)), dma((lines,)), dma((lines,)),
-            dma((lines,)), dma((lines,)), dma((lines,)),
+            slots, slots, slots, slots, pltpu.VMEM(block[1:], jnp.float32),
+            dma((groups,)), dma((groups,)), *[dma((lines, groups))] * 5,
         ],
-        compiler_params=pltpu.CompilerParams(collective_id=1, has_side_effects=True),
+        compiler_params=pltpu.CompilerParams(
+            collective_id=1, has_side_effects=True, vmem_limit_bytes=12 << 20
+        ),
         cost_estimate=comm_cost(parts, 1),
         name="reduce_rows",
     )(parts.reshape(members, *block))

time: 144 us -> 108 us (0.75)
  Pallas kernels: 100 us -> 79.3 us
  matrix products: 33.7 us -> 20.7 us
    pallas_call x2, Pallas kernels: 53.1 us -> 40.7 us  [gather_rows(): pl.pallas_call(functools.partial(gather_kernel, groups, members), out_sha...]
    pallas_call x2, Pallas kernels: 47 us -> 38.6 us  [reduce_rows(): pl.pallas_call(functools.partial(reduce_kernel, groups, members), out_sha...]
    dot_general x1, matrix products: 8.58 us -> 3.59 us  [dense_device(): jnp.einsum('rkh,fkh->rf', pre_grad, gate_weights, preferred_element_type=...]
    dot_general x1, matrix products: 5.24 us -> 2.37 us  [dense_device(): jnp.einsum('rf,hf->rh', rows_grad, down_weights, preferred_element_type=j...]
    dot_general x2, matrix products: 3.62 us -> 1.8 us  [give_back(): jnp.einsum('gst,gsf->tf', leave_table, home, preferred_element_type=jnp.f...]
  transfers between devices with their start and end apart: 2 -> 2, of which waited for: 0 -> 0; matrix products, arithmetic and copies ran while one was open for 11% -> 9% of each run, Pallas kernels for 34% -> 35%
where the time goes in v3:
time: 108 us
  Pallas kernels  79.3 us (73%)
  matrix products  20.7 us (19%)
  other arithmetic  4.06 us (4%)
  starting transfers between devices  2.02 us (2%)
  local copies, waits for them, and re-layouts  1.17 us (1%)
    pallas_call x2, Pallas kernels, gather_rows(): pl.pallas_call(functools.partial(gather_kernel, groups, members), out_sha...  40.7 us
    pallas_call x2, Pallas kernels, reduce_rows(): pl.pallas_call(functools.partial(reduce_kernel, groups, members), out_sha...  38.6 us
    dot_general x1, matrix products, dense_device(): jnp.einsum('rf,fkh->rkh', rows_in, gate_weights, preferred_element_type=j...  8.43 us
    dot_general x1, matrix products, dense_device(): jnp.dot(hidden, down_weights, preferred_element_type=jnp.float32)  4.2 us
    dot_general x1, matrix products, dense_device(): jnp.einsum('rkh,fkh->rf', pre_grad, gate_weights, preferred_element_type=...  3.59 us
    dot_general x1, matrix products, dense_device(): jnp.einsum('rf,hf->rh', rows_grad, down_weights, preferred_element_type=j...  2.37 us
  transfers between devices with their start and end apart: 2, of which 0 were waited for; matrix products, arithmetic and copies ran while one was open for 9% of the time, Pallas kernels for 35%

profile of v3, /device:TPU:0, one launch (start us, length us, event | category | flops | bytes accessed | tf_op | source)
XLA Modules:
  0.0 108.2 jit_solution(2379674812019748157)
XLA Ops:
  0.6 0.0 copy-start
  0.6 0.8 slice_reduce_fusion
  1.4 0.1 squeeze.19
  1.5 0.1 fusion.41
  1.6 0.1 reduce_window_sum.22
  1.7 0.1 copy.14
  1.8 0.0 copy-done
  1.8 0.2 convolution_convert_fusion.1.leaving
  1.9 0.0 slice-start.3
  2.0 21.7 %gather_rows.2 = bf16[8,2,16,2560]{3,2,1,0:T(8,128)(2,1)S(1)} custom-call(bf16[2,16,2560]{2,1,0:T(8,128)(2,1)S(1)} %convolution_convert_fusion.1.leaving), custom_call_target="tpu_custom_call" | custom-call | bytes 20971520 | tf_op jit(solution)/shard_map/gather_rows/pallas_call | solution.py:315
  23.7 0.0 copy-start.1
  23.7 0.0 slice-start.4
  23.7 8.4 %fusion.57 = (bf16[256,2,1024]{2,0,1:T(8,128)(2,1)}, f32[256,2,1024]{2,0,1:T(8,128)S(1)}) fusion(bf16[256,2560,1]{1,0,2:T(8,128)(2,1)S(1)} %bitcast.94, bf16[2560,2,1024]{2,1,0:T(2,128)(2,1)} %bitcast.99), kind=kOutput, calls=%fused_computation.78 | convolution fusion | flops 2684878848 | bytes 14942208 | tf_op jit(solution)/shard_map/rf,fkh->rkh/dot_general | solution.py:402
  32.1 1.5 %collective-permute-start = (bf16[256,2,1024]{2,0,1:T(8,128)(2,1)}, bf16[256,2,1024]{2,0,1:T(8,128)(2,1)}, u32[]{:S(2)}, u32[]{:S(2)}) collective-permute-start(bf16[256,2,1024]{2,0,1:T(8,128)(2,1)} %get-tuple-element.7), channel_id=1, source_target_pairs={{0,1},{1,0},{2,3},{3,2},{4,5},{5,4},{6,7},{7,6},{8,9},{9,8},{10,11... | collective-permute-start | bytes 3145736 | tf_op jit(solution)/shard_map/ppermute | solution.py:397
  33.6 0.0 copy-done.1
  33.6 0.2 convolution_convert_fusion.leaving
  33.8 19.0 %gather_rows.3 = bf16[8,2,16,2560]{3,2,1,0:T(8,128)(2,1)S(1)} custom-call(bf16[2,16,2560]{2,1,0:T(8,128)(2,1)S(1)} %convolution_convert_fusion.leaving), custom_call_target="tpu_custom_call" | custom-call | bytes 20971520 | tf_op jit(solution)/shard_map/gather_rows/pallas_call | solution.py:315
  52.8 0.0 slice-done.3
  52.8 0.0 slice-done.4
  52.9 0.0 copy-start.2
  52.9 0.0 copy-start.3
  52.9 2.4 %fusion.58 = (bf16[256,1024]{1,0:T(8,128)(2,1)}, f32[256,1024]{1,0:T(8,128)S(1)}) fusion(bf16[256,2560]{1,0:T(8,128)(2,1)S(1)} %bitcast.95, bf16[1,1024,2560]{2,1,0:T(8,128)(2,1)S(1)} %bitcast.104), kind=kOutput, calls=%fused_computation.79 | convolution fusion | flops 1342439424 | bytes 8126464 | tf_op jit(solution)/shard_map/rf,hf->rh/dot_general | solution.py:405
  55.2 0.5 collective-permute-start.1
  55.8 0.0 copy-done.2
  55.8 0.0 copy-done.3
  55.9 0.1 mul.69
  55.9 0.4 reduce_window_sum.23
  56.3 0.1 select_reduce_fusion
  56.5 0.1 mul.72
  56.5 0.0 collective-permute-done
  56.5 0.0 slice-start
  56.6 1.7 %convert_add_fusion = f32[256,2,1024]{2,0,1:T(8,128)S(1)} fusion(f32[256,2,1024]{2,0,1:T(8,128)S(1)} %get-tuple-element.8, bf16[256,2,1024]{2,0,1:T(8,128)(2,1)} %collective-permute-done), kind=kLoop, calls=%fused_computation.18 | loop fusion | flops 1048576 | bytes 5242880 | tf_op jit(solution)/shard_map/add | solution.py:398
  58.3 0.0 slice-start.1
  58.3 0.0 slice-start.2
  58.3 4.2 %fusion.17 = bf16[256,2560]{1,0:T(8,128)(2,1)S(1)} fusion(bf16[1,1024,2560]{2,1,0:T(8,128)(2,1)} %param.11, f32[256]{0:T(256)S(1)} %mul.72, f32[256,2,1024]{2,0,1:T(8,128)S(1)} %convert_add_fusion), kind=kOutput, calls=%fused_computation.11 | convolution fusion | flops 1345060864 | bytes 8651776 | tf_op jit(solution)/shard_map/dot_general | solution.py:410
  62.5 19.1 %reduce_rows.2 = bf16[2,16,2560]{2,1,0:T(8,128)(2,1)S(1)} custom-call(bf16[8,2,16,2560]{3,2,1,0:T(8,128)(2,1)S(1)} %bitcast.97), custom_call_target="tpu_custom_call" | custom-call | bytes 20971520 | tf_op jit(solution)/shard_map/reduce_rows/pallas_call | solution.py:338
  81.6 0.9 fusion.20
  82.5 0.0 collective-permute-done.1
  82.5 1.7 %fusion.36 = (bf16[256,1,1024]{2,0,1:T(8,128)(2,1)S(1)}, bf16[256,1,1024]{2,0,1:T(8,128)(2,1)S(1)}) fusion(f32[256,2,1024]{2,0,1:T(8,128)S(1)} %convert_add_fusion, f32[256]{0:T(256)S(1)} %mul.72, f32[256,1024]{1,0:T(8,128)S(1)} %get-tuple-element.10, bf16[256,1024]{1,0:T(8,128)(2,1)} %collective-permute-done.1), kind=kLoop, calls=%fused_computation.39 | loop fusion | flops 4194304 | bytes 4719616 | tf_op jit(solution)/shard_map/stack | solution.py:29
  84.2 0.0 slice-done
  84.2 0.0 slice-done.1
  84.2 0.0 slice-done.2
  84.2 3.6 %fusion.14 = bf16[256,2560]{1,0:T(8,128)(2,1)S(1)} fusion(bf16[2560,2,1024]{2,1,0:T(2,128)(2,1)S(1)} %bitcast.102, bf16[256,1,1024]{2,0,1:T(8,128)(2,1)S(1)} %get-tuple-element.6, bf16[256,1,1024]{2,0,1:T(8,128)(2,1)S(1)} %get-tuple-element.5), kind=kOutput, calls=%fused_computation.10 | convolution fusion | flops 2685534208 | bytes 12845056 | tf_op jit(solution)/shard_map/rkh,fkh->rf/dot_general | solution.py:413
  87.8 19.5 %reduce_rows.3 = bf16[2,16,2560]{2,1,0:T(8,128)(2,1)S(1)} custom-call(bf16[8,2,16,2560]{3,2,1,0:T(8,128)(2,1)S(1)} %bitcast.96), custom_call_target="tpu_custom_call" | custom-call | bytes 20971520 | tf_op jit(solution)/shard_map/reduce_rows/pallas_call | solution.py:338
  107.3 0.9 fusion.21
  (10 shorter events, 0.1 us)
Async XLA Ops:
  0.6 1.1 %copy-start = (bf16[32,2560]{1,0:T(8,128)(2,1)S(1)}, bf16[32,2560]{1,0:T(8,128)(2,1)}, u32[]{:S(2)}) copy-start(bf16[32,2560]{1,0:T(8,128)(2,1)} %param.6) | copy-start | bytes 491524
  1.9 50.9 %slice-start.3 = ((s8[5242880]{0:T(1024)(128)(4,1)}), s8[4194304]{0:T(1024)(128)(4,1)S(1)}, s32[]{:S(2)}) async-start(s8[5242880]{0:T(1024)(128)(4,1)} %bitcast.103), calls=%async_computation.3 | async-start | bytes 8388608
  23.7 10.0 %copy-start.1 = (bf16[32,2560]{1,0:T(8,128)(2,1)S(1)}, bf16[32,2560]{1,0:T(8,128)(2,1)}, u32[]{:S(2)}) copy-start(bf16[32,2560]{1,0:T(8,128)(2,1)} %param.7) | copy-start | bytes 491524
  23.7 29.2 %slice-start.4 = ((s8[5242880]{0:T(1024)(128)(4,1)}), s8[1048576]{0:T(1024)(128)(4,1)S(1)}, s32[]{:S(2)}) async-start(s8[5242880]{0:T(1024)(128)(4,1)} %bitcast.103), calls=%async_computation.4 | async-start | bytes 2097152
  32.1 24.4 %collective-permute-start = (bf16[256,2,1024]{2,0,1:T(8,128)(2,1)}, bf16[256,2,1024]{2,0,1:T(8,128)(2,1)}, u32[]{:S(2)}, u32[]{:S(2)}) collective-permute-start(bf16[256,2,1024]{2,0,1:T(8,128)(2,1)} %get-tuple-element.7), channel_id=1, source_target_pairs={{0,1},{1,0},{2,3},{3,2},{4,5},{5,4},{6,7},{7,6},{8,9},{9,8},{10,11... | collective-permute-start | bytes 3145736 | tf_op jit(solution)/shard_map/ppermute | solution.py:397
  52.9 2.9 %copy-start.2 = (f32[512,8]{0,1:T(8,128)S(1)}, f32[512,8]{0,1:T(8,128)}, u32[]{:S(2)}) copy-start(f32[512,8]{0,1:T(8,128)} %param.9) | copy-start | bytes 49156
  52.9 2.9 %copy-start.3 = (s32[512,8]{0,1:T(8,128)S(1)}, s32[512,8]{0,1:T(8,128)}, u32[]{:S(2)}) copy-start(s32[512,8]{0,1:T(8,128)} %param.8) | copy-start | bytes 49156
  55.2 27.3 %collective-permute-start.1 = (bf16[256,1024]{1,0:T(8,128)(2,1)}, bf16[256,1024]{1,0:T(8,128)(2,1)}, u32[]{:S(2)}, u32[]{:S(2)}) collective-permute-start(bf16[256,1024]{1,0:T(8,128)(2,1)} %get-tuple-element.9), channel_id=1, source_target_pairs={{0,1},{1,0},{2,3},{3,2},{4,5},{5,4},{6,7},{7,6},{8,9},{9,8},{10,11... | collective-permute-start | bytes 1572872 | tf_op jit(solution)/shard_map/ppermute | solution.py:397
  56.5 27.6 %slice-start = ((s8[10485760]{0:T(1024)(128)(4,1)}), s8[4194304]{0:T(1024)(128)(4,1)S(1)}, s32[]{:S(2)}) async-start(s8[10485760]{0:T(1024)(128)(4,1)} %bitcast.100), calls=%async_computation | async-start | bytes 8388608
  58.3 25.9 %slice-start.1 = ((s8[10485760]{0:T(1024)(128)(4,1)}), s8[4194304]{0:T(1024)(128)(4,1)S(1)}, s32[]{:S(2)}) async-start(s8[10485760]{0:T(1024)(128)(4,1)} %bitcast.100), calls=%async_computation.1 | async-start | bytes 8388608
  58.3 25.9 %slice-start.2 = ((s8[10485760]{0:T(1024)(128)(4,1)}), s8[2097152]{0:T(1024)(128)(4,1)S(1)}, s32[]{:S(2)}) async-start(s8[10485760]{0:T(1024)(128)(4,1)} %bitcast.100), calls=%async_computation.2 | async-start | bytes 4194304

commit v4 on v3

--- a/solution.py
+++ b/solution.py
@@ -47,6 +47,7 @@
 
 MESH = pl.DeviceIdType.MESH
 LANES = 2
+CUTS = 2
 
 
 def greet(groups, me, lines):
@@ -81,24 +82,24 @@
     beside = line * LANES + 1 - lane
     greet(groups, me, lines)
 
-    def pair_copy(step):
+    def pair_copy(step, cut):
         other = lax.rem(my_group + step, groups)
         return pltpu.make_async_remote_copy(
-            src_ref=leaving.at[other],
-            dst_ref=out.at[me, my_group],
-            send_sem=pair_send.at[step],
-            recv_sem=pair_recv.at[step],
+            src_ref=leaving.at[other * CUTS + cut],
+            dst_ref=out.at[me, my_group * CUTS + cut],
+            send_sem=pair_send.at[step, cut],
+            recv_sem=pair_recv.at[step, cut],
             device_id={"group": other},
             device_id_type=MESH,
         )
 
-    def pair_wait(step):
+    def pair_wait(step, cut):
         source = lax.rem(my_group + groups - step, groups)
         pltpu.make_async_remote_copy(
-            src_ref=leaving.at[source],
-            dst_ref=out.at[me, source],
-            send_sem=pair_send.at[step],
-            recv_sem=pair_recv.at[step],
+            src_ref=leaving.at[source * CUTS + cut],
+            dst_ref=out.at[me, source * CUTS + cut],
+            send_sem=pair_send.at[step, cut],
+            recv_sem=pair_recv.at[step, cut],
             device_id={"group": source},
             device_id_type=MESH,
         ).wait_recv()
@@ -122,14 +123,17 @@
     def hop_side(block, piece):
         return hop(2, block, piece, beside)
 
-    for step in range(1, groups):
-        pair_copy(step).start()
-    own = pltpu.make_async_copy(leaving.at[my_group], out.at[me, my_group], own_sem)
+    steps = [(step, cut) for step in range(groups) for cut in range(CUTS)]
+    away = steps[CUTS:]
+    for step, cut in away:
+        pair_copy(step, cut).start()
+    stay = pl.ds(my_group * CUTS, CUTS)
+    own = pltpu.make_async_copy(leaving.at[stay], out.at[me, stay], own_sem)
     own.start()
     own.wait()
 
     def visit(reach, act, arrive):
-        for step in range(groups):
+        for step, cut in steps:
             def above(block, piece):
                 arrive(block, piece)
                 pl.when(line > 0)(lambda: act(hop_down(block, piece)))
@@ -140,14 +144,14 @@
                 pl.when(line < lines - 1)(lambda: act(hop_up(block, piece)))
                 act(hop_side(block, piece))
 
-            piece = lax.rem(my_group + groups - step, groups)
+            piece = lax.rem(my_group + groups - step, groups) * CUTS + cut
             pl.when(line - reach >= 0)(functools.partial(below, me - reach * LANES, piece))
             pl.when(line + reach <= lines - 1)(
                 functools.partial(above, me + reach * LANES, piece)
             )
 
-    def visit_own(step, act):
-        piece = lax.rem(my_group + groups - step, groups)
+    def visit_own(step, cut, act):
+        piece = lax.rem(my_group + groups - step, groups) * CUTS + cut
         act(hop_side(me, piece))
         pl.when(line < lines - 1)(lambda: act(hop_up(me, piece)))
         pl.when(line > 0)(lambda: act(hop_down(me, piece)))
@@ -158,21 +162,21 @@
     def sent(copy):
         copy.wait_send()
 
-    for step in range(groups):
+    for step, cut in steps:
         if step:
-            pair_wait(step)
-        visit_own(step, begin)
+            pair_wait(step, cut)
+        visit_own(step, cut, begin)
     for reach in range(1, lines):
         visit(reach, begin, lambda block, piece: hop_side(block, piece).wait_recv())
     for place in range(lines):
-        for piece in range(groups):
+        for piece in range(groups * CUTS):
             hop_side(place * LANES + 1 - lane, piece).wait_recv()
-    for step in range(groups):
-        visit_own(step, sent)
+    for step, cut in steps:
+        visit_own(step, cut, sent)
     for reach in range(1, lines):
         visit(reach, sent, lambda block, piece: None)
-    for step in range(1, groups):
-        pair_copy(step).wait_send()
+    for step, cut in away:
+        pair_copy(step, cut).wait_send()
 
 
 def reduce_kernel(
@@ -212,10 +216,13 @@
     def down_copy(place, piece):
         return line_copy(down, down_recv, place, piece, me - LANES)
 
+    steps = [(step, cut) for step in range(1, groups + 1) for cut in range(CUTS)]
+    away = steps[:-CUTS]
+
     def far_first(above, below):
         for reach in range(lines - 1, 0, -1):
-            for step in range(groups):
-                piece = lax.rem(my_group + 1 + step, groups)
+            for step, cut in steps:
+                piece = lax.rem(my_group + step, groups) * CUTS + cut
                 pl.when(line + reach <= lines - 1)(
                     functools.partial(above, line + reach, piece)
                 )
@@ -225,8 +232,8 @@
         side_copy(place, piece).start()
 
     far_first(begin, begin)
-    for step in range(groups):
-        begin(line, lax.rem(my_group + 1 + step, groups))
+    for step, cut in steps:
+        begin(line, lax.rem(my_group + step, groups) * CUTS + cut)
 
     def pair_sum(place, piece):
         mine = parts[place * LANES + lane, piece].astype(jnp.float32)
@@ -252,19 +259,19 @@
         functools.partial(pass_on, down, down_copy, line < lines - 1),
     )
 
-    def pair_copy(step):
+    def pair_copy(step, cut):
         other = lax.rem(my_group + step, groups)
         return pltpu.make_async_remote_copy(
-            src_ref=passing.at[line, other],
-            dst_ref=home.at[my_group],
-            send_sem=pair_send.at[step],
-            recv_sem=pair_recv.at[step],
+            src_ref=passing.at[line, other * CUTS + cut],
+            dst_ref=home.at[my_group * CUTS + cut],
+            send_sem=pair_send.at[step, cut],
+            recv_sem=pair_recv.at[step, cut],
             device_id={"group": other},
             device_id_type=MESH,
         )
 
-    for step in range(1, groups + 1):
-        piece = lax.rem(my_group + step, groups)
+    for step, cut in steps:
+        piece = lax.rem(my_group + step, groups) * CUTS + cut
         side_copy(line, piece).wait_recv()
         total[...] = pair_sum(line, piece)
 
@@ -280,26 +287,26 @@
 
         if step < groups:
             passing[line, piece] = total[...].astype(passing.dtype)
-            pair_copy(step).start()
+            pair_copy(step, cut).start()
         else:
-            home[my_group] = total[...].astype(home.dtype)
-    for step in range(1, groups):
+            home[my_group * CUTS + cut] = total[...].astype(home.dtype)
+    for step, cut in away:
         source = lax.rem(my_group + groups - step, groups)
         pltpu.make_async_remote_copy(
-            src_ref=passing.at[line, source],
-            dst_ref=home.at[source],
-            send_sem=pair_send.at[step],
-            recv_sem=pair_recv.at[step],
+            src_ref=passing.at[line, source * CUTS + cut],
+            dst_ref=home.at[source * CUTS + cut],
+            send_sem=pair_send.at[step, cut],
+            recv_sem=pair_recv.at[step, cut],
             device_id={"group": source},
             device_id_type=MESH,
         ).wait_recv()
-        pair_copy(step).wait_send()
+        pair_copy(step, cut).wait_send()
     far_first(
         lambda place, piece: up_copy(place, piece).wait_send(),
         lambda place, piece: down_copy(place, piece).wait_send(),
     )
     for place in range(lines):
-        for piece in range(groups):
+        for piece in range(groups * CUTS):
             side_copy(place, piece).wait_send()
 
 
@@ -311,6 +318,7 @@
 
 def gather_rows(leaving, members):
     groups, visitors, features = leaving.shape
+    leaving = leaving.reshape(groups * CUTS, visitors // CUTS, features)
     dma = pltpu.SemaphoreType.DMA
     return pl.pallas_call(
         functools.partial(gather_kernel, groups, members),
@@ -319,8 +327,8 @@
         out_specs=pl.BlockSpec(memory_space=pltpu.VMEM),
         scratch_shapes=[
             dma(()),
-            dma((groups,)), dma((groups,)),
-            dma((3, members, groups)), dma((members, groups)),
+            dma((groups, CUTS)), dma((groups, CUTS)),
+            dma((3, members, groups * CUTS)), dma((members, groups * CUTS)),
         ],
         compiler_params=pltpu.CompilerParams(
             collective_id=0, has_side_effects=True, vmem_limit_bytes=8 << 20
@@ -331,7 +339,8 @@
 
 
 def reduce_rows(parts, groups, members):
-    block = (groups, parts.shape[0] // (groups * members), parts.shape[1])
+    pieces = groups * CUTS
+    block = (pieces, parts.shape[0] // (pieces * members), parts.shape[1])
     lines = members // LANES
     dma = pltpu.SemaphoreType.DMA
     slots = pltpu.VMEM((lines, *block), parts.dtype)
@@ -342,7 +351,7 @@
         out_specs=pl.BlockSpec(memory_space=pltpu.VMEM),
         scratch_shapes=[
             slots, slots, slots, slots, pltpu.VMEM(block[1:], jnp.float32),
-            dma((groups,)), dma((groups,)), *[dma((lines, groups))] * 5,
+            dma((groups, CUTS)), dma((groups, CUTS)), *[dma((lines, pieces))] * 5,
         ],
         compiler_params=pltpu.CompilerParams(
             collective_id=1, has_side_effects=True, vmem_limit_bytes=12 << 20
@@ -415,7 +424,7 @@
     ).astype(jnp.bfloat16)
 
     def give_back(parts):
-        home = reduce_rows(parts, groups, members)
+        home = reduce_rows(parts, groups, members).reshape(groups, visitors, features)
         return jnp.einsum(
             "gst,gsf->tf", leave_table, home, preferred_element_type=jnp.float32
         ).astype(jnp.bfloat16)

time: 108 us -> 107 us (level)
  Pallas kernels: 79.3 us -> 76.9 us
    pallas_call x2, Pallas kernels: 40.7 us -> 39 us  [gather_rows(): pl.pallas_call(functools.partial(gather_kernel, groups, members), out_sha...]
  transfers between devices with their start and end apart: 2 -> 2, of which waited for: 0 -> 1; matrix products, arithmetic and copies ran while one was open for 9% -> 9% of each run, Pallas kernels for 35% -> 35%
where the time goes in v4:
time: 107 us
  Pallas kernels  76.9 us (72%)
  matrix products  20.8 us (19%)
  other arithmetic  4.15 us (4%)
  starting transfers between devices  2.03 us (2%)
  local copies, waits for them, and re-layouts  1.17 us (1%)
    pallas_call x2, Pallas kernels, gather_rows(): pl.pallas_call(functools.partial(gather_kernel, groups, members), out_sha...  39 us
    pallas_call x2, Pallas kernels, reduce_rows(): pl.pallas_call(functools.partial(reduce_kernel, groups, members), out_sha...  37.9 us
    dot_general x1, matrix products, dense_device(): jnp.einsum('rf,fkh->rkh', rows_in, gate_weights, preferred_element_type=j...  8.43 us
    dot_general x1, matrix products, dense_device(): jnp.dot(hidden, down_weights, preferred_element_type=jnp.float32)  4.2 us
    dot_general x1, matrix products, dense_device(): jnp.einsum('rkh,fkh->rf', pre_grad, gate_weights, preferred_element_type=...  3.61 us
    dot_general x1, matrix products, dense_device(): jnp.einsum('rf,hf->rh', rows_grad, down_weights, preferred_element_type=j...  2.37 us
  transfers between devices with their start and end apart: 2, of which 1 were waited for; matrix products, arithmetic and copies ran while one was open for 9% of the time, Pallas kernels for 35%

profile of v4, /device:TPU:0, one launch (start us, length us, event | category | flops | bytes accessed | tf_op | source)
XLA Modules:
  0.0 106.7 jit_solution(10150103226068172068)
XLA Ops:
  0.6 0.0 copy-start
  0.6 0.8 slice_reduce_fusion
  1.4 0.1 squeeze.19
  1.5 0.1 fusion.41
  1.6 0.1 reduce_window_sum.22
  1.7 0.1 copy.14
  1.8 0.0 copy-done
  1.8 0.2 convolution_convert_fusion.1
  1.9 0.0 slice-start.3
  2.0 20.8 %gather_rows.2 = bf16[8,4,8,2560]{3,2,1,0:T(8,128)(2,1)S(1)} custom-call(bf16[4,8,2560]{2,1,0:T(8,128)(2,1)S(1)} %bitcast.104), custom_call_target="tpu_custom_call" | custom-call | bytes 20971520 | tf_op jit(solution)/shard_map/gather_rows/pallas_call | solution.py:323
  22.8 0.0 copy-start.1
  22.8 0.0 slice-start.4
  22.8 8.4 %fusion.57 = (bf16[256,2,1024]{2,0,1:T(8,128)(2,1)}, f32[256,2,1024]{2,0,1:T(8,128)S(1)}) fusion(bf16[256,2560,1]{1,0,2:T(8,128)(2,1)S(1)} %bitcast.98, bf16[2560,2,1024]{2,1,0:T(2,128)(2,1)} %bitcast.107), kind=kOutput, calls=%fused_computation.78 | convolution fusion | flops 2684878848 | bytes 14942208 | tf_op jit(solution)/shard_map/rf,fkh->rkh/dot_general | solution.py:411
  31.2 1.5 %collective-permute-start = (bf16[256,2,1024]{2,0,1:T(8,128)(2,1)}, bf16[256,2,1024]{2,0,1:T(8,128)(2,1)}, u32[]{:S(2)}, u32[]{:S(2)}) collective-permute-start(bf16[256,2,1024]{2,0,1:T(8,128)(2,1)} %get-tuple-element.7), channel_id=1, source_target_pairs={{0,1},{1,0},{2,3},{3,2},{4,5},{5,4},{6,7},{7,6},{8,9},{9,8},{10,11... | collective-permute-start | bytes 3145736 | tf_op jit(solution)/shard_map/ppermute | solution.py:406
  32.7 0.0 copy-done.1
  32.7 0.2 convolution_convert_fusion
  32.9 18.2 %gather_rows.3 = bf16[8,4,8,2560]{3,2,1,0:T(8,128)(2,1)S(1)} custom-call(bf16[4,8,2560]{2,1,0:T(8,128)(2,1)S(1)} %bitcast.105), custom_call_target="tpu_custom_call" | custom-call | bytes 20971520 | tf_op jit(solution)/shard_map/gather_rows/pallas_call | solution.py:323
  51.1 0.0 slice-done.3
  51.1 0.0 slice-done.4
  51.1 0.0 copy-start.2
  51.1 0.0 copy-start.3
  51.2 2.4 %fusion.58 = (bf16[256,1024]{1,0:T(8,128)(2,1)}, f32[256,1024]{1,0:T(8,128)S(1)}) fusion(bf16[256,2560]{1,0:T(8,128)(2,1)S(1)} %bitcast.99, bf16[1,1024,2560]{2,1,0:T(8,128)(2,1)S(1)} %bitcast.112), kind=kOutput, calls=%fused_computation.79 | convolution fusion | flops 1342439424 | bytes 8126464 | tf_op jit(solution)/shard_map/rf,hf->rh/dot_general | solution.py:414
  53.5 0.5 collective-permute-start.1
  54.1 0.0 copy-done.2
  54.1 0.0 copy-done.3
  54.1 0.1 mul.69
  54.2 0.4 reduce_window_sum.23
  54.6 0.1 select_reduce_fusion
  54.7 0.1 mul.72
  54.8 0.8 collective-permute-done
  55.6 0.0 slice-start
  55.6 1.7 %convert_add_fusion = f32[256,2,1024]{2,0,1:T(8,128)S(1)} fusion(f32[256,2,1024]{2,0,1:T(8,128)S(1)} %get-tuple-element.8, bf16[256,2,1024]{2,0,1:T(8,128)(2,1)} %collective-permute-done), kind=kLoop, calls=%fused_computation.18 | loop fusion | flops 1048576 | bytes 5242880 | tf_op jit(solution)/shard_map/add | solution.py:407
  57.4 0.0 slice-start.1
  57.4 0.0 slice-start.2
  57.4 4.2 %fusion.17 = bf16[256,2560]{1,0:T(8,128)(2,1)S(1)} fusion(bf16[1,1024,2560]{2,1,0:T(8,128)(2,1)} %param.11, f32[256]{0:T(256)S(1)} %mul.72, f32[256,2,1024]{2,0,1:T(8,128)S(1)} %convert_add_fusion), kind=kOutput, calls=%fused_computation.11 | convolution fusion | flops 1345060864 | bytes 8651776 | tf_op jit(solution)/shard_map/dot_general | solution.py:419
  61.6 19.2 %reduce_rows.2 = bf16[4,8,2560]{2,1,0:T(8,128)(2,1)S(1)} custom-call(bf16[8,4,8,2560]{3,2,1,0:T(8,128)(2,1)S(1)} %bitcast.101), custom_call_target="tpu_custom_call" | custom-call | bytes 20971520 | tf_op jit(solution)/shard_map/reduce_rows/pallas_call | solution.py:347
  80.9 0.9 fusion.20
  81.8 0.0 collective-permute-done.1
  81.8 1.7 %fusion.36 = (bf16[256,1,1024]{2,0,1:T(8,128)(2,1)S(1)}, bf16[256,1,1024]{2,0,1:T(8,128)(2,1)S(1)}) fusion(f32[256,2,1024]{2,0,1:T(8,128)S(1)} %convert_add_fusion, f32[256]{0:T(256)S(1)} %mul.72, f32[256,1024]{1,0:T(8,128)S(1)} %get-tuple-element.10, bf16[256,1024]{1,0:T(8,128)(2,1)} %collective-permute-done.1), kind=kLoop, calls=%fused_computation.39 | loop fusion | flops 4194304 | bytes 4719616 | tf_op jit(solution)/shard_map/stack | solution.py:29
  83.5 0.0 slice-done
  83.5 0.0 slice-done.1
  83.5 0.0 slice-done.2
  83.5 3.6 %fusion.14 = bf16[256,2560]{1,0:T(8,128)(2,1)S(1)} fusion(bf16[2560,2,1024]{2,1,0:T(2,128)(2,1)S(1)} %bitcast.110, bf16[256,1,1024]{2,0,1:T(8,128)(2,1)S(1)} %get-tuple-element.6, bf16[256,1,1024]{2,0,1:T(8,128)(2,1)S(1)} %get-tuple-element.5), kind=kOutput, calls=%fused_computation.10 | convolution fusion | flops 2685534208 | bytes 12845056 | tf_op jit(solution)/shard_map/rkh,fkh->rf/dot_general | solution.py:422
  87.1 18.6 %reduce_rows.3 = bf16[4,8,2560]{2,1,0:T(8,128)(2,1)S(1)} custom-call(bf16[8,4,8,2560]{3,2,1,0:T(8,128)(2,1)S(1)} %bitcast.100), custom_call_target="tpu_custom_call" | custom-call | bytes 20971520 | tf_op jit(solution)/shard_map/reduce_rows/pallas_call | solution.py:347
  105.8 0.9 fusion.21
  (10 shorter events, 0.1 us)
Async XLA Ops:
  0.6 1.1 %copy-start = (bf16[32,2560]{1,0:T(8,128)(2,1)S(1)}, bf16[32,2560]{1,0:T(8,128)(2,1)}, u32[]{:S(2)}) copy-start(bf16[32,2560]{1,0:T(8,128)(2,1)} %param.6) | copy-start | bytes 491524
  1.9 49.2 %slice-start.3 = ((s8[5242880]{0:T(1024)(128)(4,1)}), s8[4194304]{0:T(1024)(128)(4,1)S(1)}, s32[]{:S(2)}) async-start(s8[5242880]{0:T(1024)(128)(4,1)} %bitcast.111), calls=%async_computation.3 | async-start | bytes 8388608
  22.8 10.0 %copy-start.1 = (bf16[32,2560]{1,0:T(8,128)(2,1)S(1)}, bf16[32,2560]{1,0:T(8,128)(2,1)}, u32[]{:S(2)}) copy-start(bf16[32,2560]{1,0:T(8,128)(2,1)} %param.7) | copy-start | bytes 491524
  22.8 28.3 %slice-start.4 = ((s8[5242880]{0:T(1024)(128)(4,1)}), s8[1048576]{0:T(1024)(128)(4,1)S(1)}, s32[]{:S(2)}) async-start(s8[5242880]{0:T(1024)(128)(4,1)} %bitcast.111), calls=%async_computation.4 | async-start | bytes 2097152
  31.2 24.4 %collective-permute-start = (bf16[256,2,1024]{2,0,1:T(8,128)(2,1)}, bf16[256,2,1024]{2,0,1:T(8,128)(2,1)}, u32[]{:S(2)}, u32[]{:S(2)}) collective-permute-start(bf16[256,2,1024]{2,0,1:T(8,128)(2,1)} %get-tuple-element.7), channel_id=1, source_target_pairs={{0,1},{1,0},{2,3},{3,2},{4,5},{5,4},{6,7},{7,6},{8,9},{9,8},{10,11... | collective-permute-start | bytes 3145736 | tf_op jit(solution)/shard_map/ppermute | solution.py:406
  51.1 2.9 %copy-start.2 = (f32[512,8]{0,1:T(8,128)S(1)}, f32[512,8]{0,1:T(8,128)}, u32[]{:S(2)}) copy-start(f32[512,8]{0,1:T(8,128)} %param.9) | copy-start | bytes 49156
  51.1 3.0 %copy-start.3 = (s32[512,8]{0,1:T(8,128)S(1)}, s32[512,8]{0,1:T(8,128)}, u32[]{:S(2)}) copy-start(s32[512,8]{0,1:T(8,128)} %param.8) | copy-start | bytes 49156
  53.5 28.2 %collective-permute-start.1 = (bf16[256,1024]{1,0:T(8,128)(2,1)}, bf16[256,1024]{1,0:T(8,128)(2,1)}, u32[]{:S(2)}, u32[]{:S(2)}) collective-permute-start(bf16[256,1024]{1,0:T(8,128)(2,1)} %get-tuple-element.9), channel_id=1, source_target_pairs={{0,1},{1,0},{2,3},{3,2},{4,5},{5,4},{6,7},{7,6},{8,9},{9,8},{10,11... | collective-permute-start | bytes 1572872 | tf_op jit(solution)/shard_map/ppermute | solution.py:406
  55.6 27.8 %slice-start = ((s8[10485760]{0:T(1024)(128)(4,1)}), s8[4194304]{0:T(1024)(128)(4,1)S(1)}, s32[]{:S(2)}) async-start(s8[10485760]{0:T(1024)(128)(4,1)} %bitcast.108), calls=%async_computation | async-start | bytes 8388608
  57.4 26.1 %slice-start.1 = ((s8[10485760]{0:T(1024)(128)(4,1)}), s8[4194304]{0:T(1024)(128)(4,1)S(1)}, s32[]{:S(2)}) async-start(s8[10485760]{0:T(1024)(128)(4,1)} %bitcast.108), calls=%async_computation.1 | async-start | bytes 8388608
  57.4 26.1 %slice-start.2 = ((s8[10485760]{0:T(1024)(128)(4,1)}), s8[2097152]{0:T(1024)(128)(4,1)S(1)}, s32[]{:S(2)}) async-start(s8[10485760]{0:T(1024)(128)(4,1)} %bitcast.108), calls=%async_computation.2 | async-start | bytes 4194304
